TPU v7x, 256 devices: a whole 4x4x8 slice. The times are simulated.
256 devices in a mesh: segment: 2 (over core), rows: 32 (over z, x), dp: 4 (over y).
Axes of the slice: x: 4, y: 4, z: 8, core: 2. Of those that a mesh axis runs over, the one named last changes fastest.
Arguments:
- coarse: bfloat16 [8, 100, 384, 256], P(('segment', 'dp'), None, 'rows'), may hold values from -6 to 6
- target: bfloat16 [8, 64, 384, 256], P(('segment', 'dp'), None, 'rows'), may hold values from -6 to 6
- noise: bfloat16 [8, 32, 64, 64, 144], P(('segment', 'dp'), 'rows'), may hold values from -6 to 6
- regions: int32 [8, 32, 32, 4], P(('segment', 'dp')), may hold values from 0 to 244, as said below
- reg_conv: bfloat16 [128, 900], replicated, may hold values from -0.1875 to 0.1875
- reg_out: bfloat16 [64, 128], replicated, may hold values from -0.5 to 0.5
- conv_one: bfloat16 [128, 1152], replicated, may hold values from -0.1875 to 0.1875
- conv_two: bfloat16 [128, 1152], replicated, may hold values from -0.1875 to 0.1875
- out_proj: bfloat16 [64, 128], replicated, may hold values from -0.5 to 0.5
- step_embed: float32 [32, 128], replicated, may hold values from -3 to 3
Outputs:
- mean_field: bfloat16 [8, 64, 384, 256], P(('segment', 'dp'), None, 'rows')
- owner_loss: float32 [8, 32], P(('segment', 'dp'), 'rows')
- grad_conv_one: float32 [128, 1152], replicated
- grad_conv_two: float32 [128, 1152], replicated
- grad_out_proj: float32 [64, 128], replicated
- grad_embed: float32 [32, 128], replicated
Inputs may be any that keep to these rules, and one draw needn't show every extreme that they name: `regions`: for sample s, strip i and entry k: entry 0 is the patch's row offset within strip i (0 on the last strip), entry 1 its first column, at most 244, entry 2 its owner, entry 3 its noise level below 32. Every owner receives 2 * 32, 32 or 16 patches of a sample; for each owner with 64 there is one with 32 and two with 16. No strip lists more than 2 patches for one owner, and some strip lists exactly 2 for one owner.
All inputs are finite; a program needn't handle non-finite values.
Results may differ from a plain program's by a relative error of at most 0.0048.
Values may be sent and summed in bfloat16 or wider, within the bound.
A program may use at most 192 MiB of HBM per device.

v0:
```python
import math

import jax
import jax.numpy as jnp
from jax import lax
from jax.sharding import PartitionSpec as P

PATCH = 12


TAPS = ((-1, -1), (-1, 0), (-1, 1), (0, -1), (0, 0), (0, 1), (1, -1), (1, 0), (1, 1))


def padded_2(cells, sides, width):
    for axis, dim in sides:
        count = lax.axis_size(axis)
        ends = count - 1
        head = lax.slice_in_dim(cells, 0, width, axis=dim)
        tail = lax.slice_in_dim(cells, cells.shape[dim] - width, cells.shape[dim], axis=dim)
        cells = jnp.concatenate(
            [
                lax.ppermute(tail, axis, [(i, (i + 1) % count) for i in range(ends)]),
                cells,
                lax.ppermute(head, axis, [((i + 1) % count, i) for i in range(ends)]),
            ],
            axis=dim,
        )
    return cells


def shifted_2(block, axis, distance):
    devices = range(lax.axis_size(axis))
    route = [(i - distance, i) for i in devices if i - distance in devices]
    return lax.ppermute(block, axis, route)


def shifted(values, row_step, col_step, stride):
    length = values.shape[-1]
    margin = stride + 1
    widths = [(0, 0)] * (values.ndim - 1) + [(margin, margin)]
    padded = jnp.pad(values, widths)
    offset = margin + row_step * stride + col_step
    moved = lax.slice_in_dim(padded, offset, offset + length, axis=values.ndim - 1)
    column = jnp.arange(length, dtype=jnp.int32) % stride + col_step
    inside = (column >= 0) & (column < stride)
    return jnp.where(inside, moved, jnp.zeros((), moved.dtype))


def columns(values, stride):
    return jnp.concatenate(
        [shifted(values, row_step, col_step, stride) for row_step, col_step in TAPS], axis=-2
    )


def fold(gradients, stride):
    width = gradients.shape[-2] // 9
    result = jnp.zeros(gradients.shape[:-2] + (width, gradients.shape[-1]), jnp.float32)
    for position, (row_step, col_step) in enumerate(TAPS):
        piece = gradients[..., position * width : (position + 1) * width, :]
        result = result + shifted(piece, -row_step, -col_step, stride)
    return result


def noise_levels(level_count):
    steps_f = jnp.arange(level_count, dtype=jnp.float32)
    return 0.1 * jnp.exp(steps_f * (math.log(100.0) / (level_count - 1)))


def silu_slope(values):
    gate = jax.nn.sigmoid(values)
    return gate * (1.0 + values * (1.0 - gate))


def product(form, left, right):
    return jnp.einsum(form, left, right, preferred_element_type=jnp.float32)


def regress(grid_rows, reg_conv, reg_out):
    channels, height, width = grid_rows.shape
    flat = grid_rows.reshape(channels, height * width)
    hidden = product("ok,kp->op", reg_conv, columns(flat, width))
    activated = jax.nn.silu(hidden).astype(jnp.bfloat16)
    mean_flat = product("co,op->cp", reg_out, activated).astype(jnp.bfloat16)
    return mean_flat.reshape(reg_out.shape[0], height, width)


def patch_block(mean_part, target_part, noise_part, step_ids, in_use, weights):
    conv_one, conv_two, out_proj, step_embed = weights
    stride = PATCH
    level_count = step_embed.shape[0]
    sigma_table = noise_levels(level_count)
    step_hot = (step_ids[:, None] == jnp.arange(level_count, dtype=jnp.int32)[None, :]).astype(
        jnp.float32
    )
    sigma = jnp.sum(step_hot * sigma_table[None, :], axis=1)
    sigma_sq = sigma * sigma + 1.0
    scale_in = (1.0 / jnp.sqrt(sigma_sq))[:, None, None]
    scale_skip = (1.0 / sigma_sq)[:, None, None]
    scale_out = (sigma / jnp.sqrt(sigma_sq))[:, None, None]
    weight_loss = sigma_sq / (sigma * sigma)
    mean_float = mean_part.astype(jnp.float32)
    residual = target_part.astype(jnp.float32) - mean_float
    noisy = residual + sigma[:, None, None] * noise_part.astype(jnp.float32)
    inputs = jnp.concatenate([scale_in * noisy, mean_float], axis=1).astype(jnp.bfloat16)
    cols_in = columns(inputs, stride)
    embedded = jnp.sum(step_hot[:, :, None] * step_embed[None, :, :], axis=1)
    pre_one = product("ok,bkp->bop", conv_one, cols_in) + embedded[:, :, None]
    act_one = jax.nn.silu(pre_one).astype(jnp.bfloat16)
    cols_one = columns(act_one, stride)
    pre_two = product("ok,bkp->bop", conv_two, cols_one)
    act_two = jax.nn.silu(pre_two).astype(jnp.bfloat16)
    output = product("co,bop->bcp", out_proj, act_two)
    error = scale_skip * noisy + scale_out * output - residual
    losses = weight_loss * jnp.mean(error * error, axis=(1, 2)) * in_use
    factor = 2.0 * weight_loss * in_use / (error.shape[1] * error.shape[2])
    grad_output = (factor[:, None, None] * scale_out * error).astype(jnp.bfloat16)
    grad_proj = product("bcp,bop->co", grad_output, act_two)
    grad_act_two = product("co,bcp->bop", out_proj, grad_output)
    grad_pre_two = (grad_act_two * silu_slope(pre_two)).astype(jnp.bfloat16)
    grad_two = product("bop,bkp->ok", grad_pre_two, cols_one)
    grad_cols = product("ok,bop->bkp", conv_two, grad_pre_two)
    grad_act_one = fold(grad_cols, stride)
    grad_pre_one = (grad_act_one * silu_slope(pre_one)).astype(jnp.bfloat16)
    grad_one = product("bop,bkp->ok", grad_pre_one, cols_in)
    pixel_sums = jnp.sum(grad_pre_one, axis=2, dtype=jnp.float32)
    grad_table = jnp.sum(step_hot[:, :, None] * pixel_sums[:, None, :], axis=0)
    return (losses, (grad_one, grad_two, grad_proj, grad_table))


def run_blocks(mean_part, target_part, noise_part, step_ids, in_use, weights):
    patch_count = mean_part.shape[0]
    blocks = patch_count // 4

    def regroup(values):
        return values.reshape((blocks, 4) + values.shape[1:])

    def advance(running, group_block):
        losses, gradients = patch_block(
            group_block[0], group_block[1], group_block[2], group_block[3], group_block[4], weights
        )
        summed = (
            running[0] + gradients[0],
            running[1] + gradients[1],
            running[2] + gradients[2],
            running[3] + gradients[3],
        )
        return (summed, losses)

    initial = (
        jnp.zeros(weights[0].shape, jnp.float32),
        jnp.zeros(weights[1].shape, jnp.float32),
        jnp.zeros(weights[2].shape, jnp.float32),
        jnp.zeros(weights[3].shape, jnp.float32),
    )
    stacked = (
        regroup(mean_part),
        regroup(target_part),
        regroup(noise_part),
        regroup(step_ids),
        regroup(in_use),
    )
    gradients, losses = lax.scan(advance, initial, stacked)
    return (losses.reshape(patch_count), gradients)


def owner_tables(region_rows, strips):
    owners = region_rows[:, :, 2]
    owner_hot = (owners[:, :, None] == jnp.arange(strips, dtype=jnp.int32)[None, None, :]).astype(
        jnp.int32
    )
    pair_rank = jnp.sum((jnp.cumsum(owner_hot, axis=1) - owner_hot) * owner_hot, axis=2)
    flat_hot = owner_hot.reshape(-1, strips)
    owner_slot = jnp.sum((jnp.cumsum(flat_hot, axis=0) - flat_hot) * flat_hot, axis=1).reshape(
        owners.shape
    )
    return (owners, pair_rank, owner_slot)


def owned_slots(region_rows, owners, pair_rank, owner_slot, strip_index, capacity, most, height):
    strips = region_rows.shape[0]
    slot_hits = (
        (owners == strip_index)[:, :, None]
        & (owner_slot[:, :, None] == jnp.arange(most, dtype=jnp.int32)[None, None, :])
    ).astype(jnp.int32)
    strip_ids = jnp.arange(strips, dtype=jnp.int32)[:, None]
    recv_index = jnp.sum(slot_hits * (strip_ids * capacity + pair_rank)[:, :, None], axis=(0, 1))
    in_use = jnp.sum(slot_hits, axis=(0, 1)).astype(jnp.float32)
    step_ids = jnp.sum(slot_hits * region_rows[:, :, 3][:, :, None], axis=(0, 1))
    row_at = jnp.sum(
        slot_hits * (strip_ids * height + region_rows[:, :, 0])[:, :, None], axis=(0, 1)
    )
    col_at = jnp.sum(slot_hits * region_rows[:, :, 1][:, :, None], axis=(0, 1))
    return (recv_index, in_use, step_ids, row_at, col_at)


def cut_patches(source_grid, row_at, col_at, height):
    zero_index = jnp.zeros((), jnp.int32)

    def cut(row_start, col_start):
        piece = lax.dynamic_slice(
            source_grid,
            (zero_index, zero_index, row_start, col_start),
            (2, source_grid.shape[1], height, height),
        )
        return piece.reshape(2, source_grid.shape[1], height * height)

    return jax.vmap(cut)(row_at, col_at)


def per_device(
    coarse, target, noise, regions, reg_conv, reg_out, conv_one, conv_two, out_proj, step_embed
):
    strips = lax.axis_size("rows")
    strip_index = lax.axis_index("rows")
    region_rows = regions[0]
    per_strip = region_rows.shape[1]
    capacity = max(2, (2 * per_strip + strips - 1) // strips)
    most = 2 * per_strip
    weights = (conv_one, conv_two, out_proj, step_embed)
    rimmed = padded_2(coarse, (("rows", 2),), 1)
    mean_strip = regress(rimmed[0], reg_conv, reg_out)[:, 1:-1]
    height = mean_strip.shape[1]
    pair_strip = jnp.stack([mean_strip, target[0]])
    owners, pair_rank, owner_slot = owner_tables(region_rows, strips)
    own_regions = lax.dynamic_index_in_dim(region_rows, strip_index, 0, keepdims=False)
    own_pairs = lax.dynamic_index_in_dim(pair_rank, strip_index, 0, keepdims=False)
    slot_noise = noise[0, 0]
    below = shifted_2(pair_strip[:, :, : height - 1], "rows", -1)
    extended = jnp.concatenate([pair_strip, below], axis=2)
    patches = cut_patches(extended, own_regions[:, 0], own_regions[:, 1], height)
    outgoing = jnp.zeros((strips, capacity) + patches.shape[1:], patches.dtype)
    outgoing = outgoing.at[own_regions[:, 2], own_pairs].set(patches)
    received = lax.all_to_all(outgoing, "rows", split_axis=0, concat_axis=0, tiled=True)
    flat_recv = received.reshape((strips * capacity,) + patches.shape[1:])
    recv_index, in_use, step_ids, row_at, col_at = owned_slots(
        region_rows, owners, pair_rank, owner_slot, strip_index, capacity, most, height
    )
    gathered = jnp.take(flat_recv, recv_index, axis=0)
    losses, gradients = run_blocks(
        gathered[:, 0], gathered[:, 1], slot_noise, step_ids, in_use, weights
    )
    owner_total = jnp.sum(losses)
    totals = lax.psum(
        (gradients[0], gradients[1], gradients[2], gradients[3]), ("segment", "rows", "dp")
    )
    return (mean_strip[None], owner_total.reshape(1, 1), totals[0], totals[1], totals[2], totals[3])


def solution(mesh):
    placed = (
        P(("segment", "dp"), None, "rows", None),
        P(("segment", "dp"), None, "rows", None),
        P(("segment", "dp"), "rows", None, None, None),
        P(("segment", "dp"), None, None, None),
        P(),
        P(),
        P(),
        P(),
        P(),
        P(),
    )
    return jax.shard_map(
        per_device,
        mesh=mesh,
        in_specs=placed,
        out_specs=(
            P(("segment", "dp"), None, "rows", None),
            P(("segment", "dp"), "rows"),
            P(),
            P(),
            P(),
            P(),
        ),
        check_vma=False,
    )
```

profile of v0, /device:TPU:1, one launch (start us, length us, event | category | flops | bytes accessed | tf_op | source)
XLA Modules:
  0.0 850.0 jit_solution(5382771631686754666)
XLA Ops:
  8.1 3.9 collective-permute-start
  13.4 3.2 copy.114
  18.2 4.4 slice_select_fusion.1
  22.6 41.7 %concatenate.38 = bf16[900,3584]{1,0:T(8,128)(2,1)} concatenate(bf16[100,3584]{1,0:T(8,128)(2,1)} %get-tuple-element.387, bf16[100,3584]{1,0:T(8,128)(2,1)} %get-tuple-element.390, bf16[100,3584]{1,0:T(8,128)(2,1)} %get-tuple-element.380, bf16[100,3584]{1,0:T(8,128)(2,1)} %get-tuple-element.388, bf16[100,3584]{1,0:T(8,128)(2,1)} %get-tuple-element.391, ...), dimensions={0} | concatenate | bytes 12902400 | tf_op jit(solution)/shard_map/concatenate | solution.py:50
  64.3 5.4 fusion.29
  71.1 3.2 copy.113
  74.4 4.9 pad_maximum_fusion.2
  79.3 4.6 copy.115
  87.4 16.0 %collective-permute-done.2 = bf16[2,64,11,256]{3,1,2,0:T(8,128)(2,1)} collective-permute-done((bf16[2,64,11,256]{3,1,2,0:T(8,128)(2,1)}, bf16[2,64,11,256]{3,1,2,0:T(8,128)(2,1)}, u32[]{:S(2)}, u32[]{:S(2)}) %collective-permute-start.2) | collective-permute-done | bytes 720928 | tf_op jit(solution)/shard_map/ppermute | solution.py:34
  103.4 4.7 copy.116
  108.1 8.1 pad_maximum_fusion.1
  116.1 8.6 %gather_fusion = bf16[32,2,64,12,12]{2,1,4,3,0:T(2,128)(2,1)S(1)} fusion(bf16[2,64,23,256]{1,0,3,2:T(2,128)(2,1)} %pad_maximum_fusion.1, s32[32]{0:T(128)S(1)} %get-tuple-element.398), kind=kCustom, calls=%fused_computation | custom fusion | bytes 2359808 | tf_op jit(solution)/shard_map/vmap()/gather | solution.py:200
  124.8 3.9 copy.117
  131.2 5.8 scatter_fusion
  137.0 14.2 %all-to-all-start = ((bf16[32,2,2,64,144]{4,3,2,1,0:T(8,128)(2,1)}), bf16[32,2,2,64,144]{4,3,2,1,0:T(8,128)(2,1)}, u32[]{:S(2)}, u32[]{:S(2)}) async-start(bf16[32,2,2,64,144]{4,3,2,1,0:T(8,128)(2,1)} %scatter_fusion), calls=%async_computation | async-start | bytes 8388608 | tf_op jit(solution)/shard_map/all_to_all | solution.py:233
  151.6 9.0 %reduce-window.6 = s32[32,8,128]{2,1,0:T(8,128)S(1)} reduce-window(s32[32,8,128]{2,1,0:T(8,128)S(1)} %fusion.38, s32[]{:T(128)} %constant.269.clone.1), window={size=1x1x128 pad=0_0x0_0x127_0}, to_apply=%region_0.1 | reduce-window | flops 4161536 | bytes 262148 | tf_op jit(solution)/shard_map/reduce-window
  162.2 79.8 %all-to-all-done = bf16[32,2,2,64,144]{4,3,2,1,0:T(8,128)(2,1)} async-done(((bf16[32,2,2,64,144]{4,3,2,1,0:T(8,128)(2,1)}), bf16[32,2,2,64,144]{4,3,2,1,0:T(8,128)(2,1)}, u32[]{:S(2)}, u32[]{:S(2)}) %all-to-all-start) | async-done | bytes 2359328 | tf_op jit(solution)/shard_map/all_to_all | solution.py:233
  242.1 5.0 gather_fusion.1
  252.3 328.0 %while.21 = (s32[]{:T(128)}, f32[128,1152]{1,0:T(8,128)}, f32[128,1152]{1,0:T(8,128)}, f32[64,128]{1,0:T(8,128)S(1)}, f32[32,128]{1,0:T(8,128)S(1)}, /*index=5*/...) while((s32[]{:T(128)}, f32[128,1152]{1,0:T(8,128)}, ...), condition=%wide.region_15.16_spmd.clone, body=%wide.region_9.15_spmd.clone.sunk | while | flops 884677568 | bytes 48410204 | solution.py:162
  284.0 2.8 fusion.117
  304.6 2.8 fusion.117
  345.7 2.8 fusion.117
  366.3 2.8 fusion.117
  407.4 2.8 fusion.117
  428.0 2.8 fusion.117
  448.5 2.8 fusion.117
  469.1 2.8 fusion.117
  489.6 2.8 fusion.117
  530.8 2.8 fusion.117
  551.3 2.8 fusion.117
  581.6 79.5 %all-reduce.11 = (f32[64,128]{1,0:T(8,128)}, f32[32,128]{1,0:T(8,128)}) all-reduce(f32[64,128]{1,0:T(8,128)S(1)} %get-tuple-element.201, f32[32,128]{1,0:T(8,128)S(1)} %get-tuple-element.202), channel_id=1, replica_groups=mesh['segment'=2,'rows'=32,'dp'=4] {'segment','rows','dp'}, use_global_device_ids=true, to_apply=%region_19.20 | all-reduce | flops 12288 | bytes 98304 | tf_op jit(solution)/shard_map/psum | solution.py:243
  661.1 178.3 %all-reduce.15.cloned.1.call-done = (f32[128,1152]{1,0:T(8,128)}, f32[128,1152]{1,0:T(8,128)}) async-done(((f32[128,1152]{1,0:T(8,128)}, f32[128,1152]{1,0:T(8,128)}), (f32[128,1152]{1,0:T(8,128)}, f32[128,1152]{1,0:T(8,128)})) %all-reduce.15.cloned.1.call-update) | async-done | bytes 1179664 | tf_op jit(solution)/shard_map/psum | solution.py:243
  (909 shorter events, 316.4 us)
Async XLA Ops:
  7.2 57.1 %copy-start = (bf16[128,900]{0,1:T(8,128)(2,1)S(1)}, bf16[128,900]{0,1:T(8,128)(2,1)}, u32[]{:S(2)}) copy-start(bf16[128,900]{0,1:T(8,128)(2,1)} %param.16) | copy-start | bytes 691204
  7.2 10.3 %copy-start.9 = (bf16[1,100,12,256]{3,1,2,0:T(8,128)(2,1)S(1)}, bf16[1,100,12,256]{3,1,2,0:T(8,128)(2,1)}, u32[]{:S(2)}) copy-start(bf16[1,100,12,256]{3,1,2,0:T(8,128)(2,1)} %param.12) | copy-start | bytes 1843204
  8.1 9.4 %collective-permute-start = (bf16[1,100,1,256]{3,1,2,0:T(8,128)(2,1)S(1)}, bf16[1,100,1,256]{3,1,2,0:T(8,128)(2,1)S(1)}, u32[]{:S(2)}, u32[]{:S(2)}) collective-permute-start(bf16[1,100,1,256]{3,1,2,0:T(8,128)(2,1)S(1)} %get-tuple-element.393), channel_id=1, source_target_pairs={{0,4},{4,8},{8,12},{12,16},{16,20},{20,24},{24,28},{28,32},{32,36}... | collective-permute-start | bytes 153608 | tf_op jit(solution)/shard_map/ppermute | solution.py:22
  12.1 5.4 collective-permute-start.1
  22.6 41.7 %copy-start.12 = (bf16[64,128]{1,0:T(8,128)(2,1)S(1)}, bf16[64,128]{1,0:T(8,128)(2,1)}, u32[]{:S(2)}) copy-start(bf16[64,128]{1,0:T(8,128)(2,1)} %param.17) | copy-start | bytes 49156
  83.9 19.5 %collective-permute-start.2 = (bf16[2,64,11,256]{3,1,2,0:T(8,128)(2,1)}, bf16[2,64,11,256]{3,1,2,0:T(8,128)(2,1)}, u32[]{:S(2)}, u32[]{:S(2)}) collective-permute-start(bf16[2,64,11,256]{3,1,2,0:T(8,128)(2,1)} %copy.115), channel_id=1, source_target_pairs={{4,0},{8,4},{12,8},{16,12},{20,16},{24,20},{28,24},{32,28},{36,32}... | collective-permute-start | bytes 2162696 | tf_op jit(solution)/shard_map/ppermute | solution.py:34
  128.7 2.5 copy-start.7
  137.0 105.1 %all-to-all-start = ((bf16[32,2,2,64,144]{4,3,2,1,0:T(8,128)(2,1)}), bf16[32,2,2,64,144]{4,3,2,1,0:T(8,128)(2,1)}, u32[]{:S(2)}, u32[]{:S(2)}) async-start(bf16[32,2,2,64,144]{4,3,2,1,0:T(8,128)(2,1)} %scatter_fusion), calls=%async_computation | async-start | bytes 8388608 | tf_op jit(solution)/shard_map/all_to_all | solution.py:233
  151.2 688.2 %all-reduce.15.cloned.1.call-start = ((), (), s32[]{:S(2)}) async-start(), calls=%async_computation.1 | async-start | bytes 2359296 | tf_op jit(solution)/shard_map/psum | solution.py:243
  249.7 2.6 copy-start.8
  249.7 2.6 copy-start.10
  249.7 2.6 copy-start.11
  259.7 2.9 copy-start.2
  262.7 1.8 copy-start.3
  279.2 2.9 copy-start.2
  282.2 1.8 copy-start.3
  299.8 2.9 copy-start.2
  302.7 1.8 copy-start.3
  320.4 2.9 copy-start.2
  340.9 2.9 copy-start.2
  361.5 2.9 copy-start.2
  382.1 2.9 copy-start.2
  402.6 2.9 copy-start.2
  423.2 2.9 copy-start.2
  443.7 2.9 copy-start.2
  464.3 2.9 copy-start.2
  484.9 2.9 copy-start.2
  505.4 2.9 copy-start.2
  526.0 2.9 copy-start.2
  546.6 2.9 copy-start.2
  567.1 2.9 copy-start.2
  580.3 262.9 %copy-start.1 = (bf16[128,900]{0,1:T(8,128)(2,1)S(1)}, bf16[128,900]{0,1:T(8,128)(2,1)}, u32[]{:S(2)}) copy-start(bf16[128,900]{0,1:T(8,128)(2,1)} %param.16) | copy-start | bytes 691204
  (61 other events, 84.2 us)
Sparse Core Ops, SparseCore 0:
  580.4 258.8 all-reduce.14
where the time goes:
time: 859 us; the launch traced here: 850 us
  waiting for transfers between devices  274 us (32%)
  matrix products  190 us (22%)
  local copies, waits for them, and re-layouts  148 us (17%)
  other arithmetic  119 us (14%)
  blocking collectives  79.5 us (9%)
  starting transfers between devices  21.1 us (2%)
  between operations  14.3 us (2%)
    dot_general x129, matrix products, product(): return jnp.einsum(form, left, right, preferred_element_type=jnp.float32)  190 us
    psum x1, waiting for transfers between devices, per_device(): lax.psum((gradients[0], gradients[1], gradients[2], gradients[3]), ('segm...  178 us
    all_to_all x1, waiting for transfers between devices, per_device(): lax.all_to_all(outgoing, 'rows', split_axis=0, concat_axis=0, tiled=True)  79.8 us
    psum x1, blocking collectives, per_device(): lax.psum((gradients[0], gradients[1], gradients[2], gradients[3]), ('segm...  79.5 us
    concatenate x1, local copies, waits for them, and re-layouts, columns(): jnp.concatenate([shifted(values, row_step, col_step, stride) for row_step...  41.7 us
    while x256, other arithmetic  34.1 us
    another operation x19, other arithmetic  27.5 us
    dynamic_update_slice x16, local copies, waits for them, and re-layouts, run_blocks(): gradients, losses = lax.scan(advance, initial, stacked)  21.3 us
  transfers between devices with their start and end apart: 5, of which 3 were waited for; matrix products, arithmetic and copies ran while one was open for 2% of the time, Pallas kernels for 0%

commit v1 on v0

--- a/solution.py
+++ b/solution.py
@@ -176,21 +176,12 @@
     return (owners, pair_rank, owner_slot)
 
 
-def owned_slots(region_rows, owners, pair_rank, owner_slot, strip_index, capacity, most, height):
-    strips = region_rows.shape[0]
-    slot_hits = (
+def noise_routes(region_rows, owners, pair_rank, owner_slot, strip_index, capacity):
+    hits = (
         (owners == strip_index)[:, :, None]
-        & (owner_slot[:, :, None] == jnp.arange(most, dtype=jnp.int32)[None, None, :])
+        & (pair_rank[:, :, None] == jnp.arange(capacity, dtype=jnp.int32)[None, None, :])
     ).astype(jnp.int32)
-    strip_ids = jnp.arange(strips, dtype=jnp.int32)[:, None]
-    recv_index = jnp.sum(slot_hits * (strip_ids * capacity + pair_rank)[:, :, None], axis=(0, 1))
-    in_use = jnp.sum(slot_hits, axis=(0, 1)).astype(jnp.float32)
-    step_ids = jnp.sum(slot_hits * region_rows[:, :, 3][:, :, None], axis=(0, 1))
-    row_at = jnp.sum(
-        slot_hits * (strip_ids * height + region_rows[:, :, 0])[:, :, None], axis=(0, 1)
-    )
-    col_at = jnp.sum(slot_hits * region_rows[:, :, 1][:, :, None], axis=(0, 1))
-    return (recv_index, in_use, step_ids, row_at, col_at)
+    return jnp.sum(hits * owner_slot[:, :, None], axis=1)
 
 
 def cut_patches(source_grid, row_at, col_at, height):
@@ -212,38 +203,47 @@
 ):
     strips = lax.axis_size("rows")
     strip_index = lax.axis_index("rows")
+    sample_count = lax.axis_size("segment") * lax.axis_size("dp")
+    sample_index = lax.axis_index("segment") * lax.axis_size("dp") + lax.axis_index("dp")
     region_rows = regions[0]
     per_strip = region_rows.shape[1]
     capacity = max(2, (2 * per_strip + strips - 1) // strips)
-    most = 2 * per_strip
     weights = (conv_one, conv_two, out_proj, step_embed)
+    owners, pair_rank, owner_slot = owner_tables(region_rows, strips)
+    send_slot = noise_routes(region_rows, owners, pair_rank, owner_slot, strip_index, capacity)
+    outgoing = jnp.take(noise[0, 0], send_slot.reshape(-1), axis=0)
+    outgoing = outgoing.reshape((strips, capacity) + outgoing.shape[1:])
+    received = lax.all_to_all(outgoing, "rows", split_axis=0, concat_axis=0, tiled=True)
     rimmed = padded_2(coarse, (("rows", 2),), 1)
     mean_strip = regress(rimmed[0], reg_conv, reg_out)[:, 1:-1]
     height = mean_strip.shape[1]
     pair_strip = jnp.stack([mean_strip, target[0]])
-    owners, pair_rank, owner_slot = owner_tables(region_rows, strips)
     own_regions = lax.dynamic_index_in_dim(region_rows, strip_index, 0, keepdims=False)
     own_pairs = lax.dynamic_index_in_dim(pair_rank, strip_index, 0, keepdims=False)
-    slot_noise = noise[0, 0]
     below = shifted_2(pair_strip[:, :, : height - 1], "rows", -1)
     extended = jnp.concatenate([pair_strip, below], axis=2)
     patches = cut_patches(extended, own_regions[:, 0], own_regions[:, 1], height)
-    outgoing = jnp.zeros((strips, capacity) + patches.shape[1:], patches.dtype)
-    outgoing = outgoing.at[own_regions[:, 2], own_pairs].set(patches)
-    received = lax.all_to_all(outgoing, "rows", split_axis=0, concat_axis=0, tiled=True)
-    flat_recv = received.reshape((strips * capacity,) + patches.shape[1:])
-    recv_index, in_use, step_ids, row_at, col_at = owned_slots(
-        region_rows, owners, pair_rank, owner_slot, strip_index, capacity, most, height
-    )
-    gathered = jnp.take(flat_recv, recv_index, axis=0)
+    flat_recv = received.reshape((strips * capacity,) + received.shape[2:])
+    patch_noise = jnp.take(flat_recv, own_regions[:, 2] * capacity + own_pairs, axis=0)
+    in_use = jnp.ones((per_strip,), jnp.float32)
     losses, gradients = run_blocks(
-        gathered[:, 0], gathered[:, 1], slot_noise, step_ids, in_use, weights
-    )
-    owner_total = jnp.sum(losses)
-    totals = lax.psum(
-        (gradients[0], gradients[1], gradients[2], gradients[3]), ("segment", "rows", "dp")
-    )
-    return (mean_strip[None], owner_total.reshape(1, 1), totals[0], totals[1], totals[2], totals[3])
+        patches[:, 0], patches[:, 1], patch_noise, own_regions[:, 3], in_use, weights
+    )
+    owner_hot = (own_regions[:, 2][:, None] == jnp.arange(strips, dtype=jnp.int32)[None, :])
+    owner_part = jnp.sum(owner_hot.astype(jnp.float32) * losses[:, None], axis=0)
+    sample_hot = (jnp.arange(sample_count, dtype=jnp.int32) == sample_index).astype(jnp.float32)
+    owner_table = sample_hot[:, None] * owner_part[None, :]
+    pieces = (gradients[0], gradients[1], gradients[2], gradients[3], owner_table)
+    flat = jnp.concatenate([piece.reshape(-1) for piece in pieces])
+    summed = lax.psum(flat, ("segment", "rows", "dp"))
+    results = []
+    offset = 0
+    for piece in pieces:
+        results.append(summed[offset : offset + piece.size].reshape(piece.shape))
+        offset += piece.size
+    table = results[4]
+    owner_total = lax.dynamic_slice(table, (sample_index, strip_index), (1, 1))
+    return (mean_strip[None], owner_total, results[0], results[1], results[2], results[3])
 
 
 def solution(mesh):

time: 859 us -> 627 us (0.73)
  matrix products: 190 us -> 99.6 us
  blocking collectives: 79.5 us -> 0 us
  other arithmetic: 119 us -> 81.4 us
  local copies, waits for them, and re-layouts: 148 us -> 128 us
    dot_general x129 -> x65, matrix products: 190 us -> 99.6 us  [product(): return jnp.einsum(form, left, right, preferred_element_type=jnp.float32)]
    psum x1, waiting for transfers between devices: 178 us -> 262 us  [per_device(): summed = lax.psum(flat, ('segment', 'rows', 'dp'))]
    all_to_all x1, waiting for transfers between devices: 79.8 us -> 0.01 us  [per_device(): lax.all_to_all(outgoing, 'rows', split_axis=0, concat_axis=0, tiled=True)]
    psum x1 -> x0, blocking collectives: 79.5 us -> none  [per_device(): lax.psum((gradients[0], gradients[1], gradients[2], gradients[3]), ('segm...]
    while x256 -> x128, other arithmetic: 34.1 us -> 17 us
    dynamic_update_slice x16 -> x8, local copies, waits for them, and re-layouts: 21.3 us -> 10.4 us  [run_blocks(): gradients, losses = lax.scan(advance, initial, stacked)]
    reduce_sum x16 -> x8, other arithmetic: 20.2 us -> 9.95 us  [patch_block(): pixel_sums = jnp.sum(grad_pre_one, axis=2, dtype=jnp.float32)]
    another operation x19 -> x11, other arithmetic: 27.5 us -> 18.3 us
  transfers between devices with their start and end apart: 5 -> 5, of which waited for: 3 -> 2; matrix products, arithmetic and copies ran while one was open for 2% -> 20% of each run, Pallas kernels for 0% -> 0%
where the time goes in v1:
time: 627 us; the launch traced here: 622 us
  waiting for transfers between devices  276 us (44%)
  local copies, waits for them, and re-layouts  128 us (20%)
  matrix products  99.6 us (16%)
  other arithmetic  81.4 us (13%)
  starting transfers between devices  20 us (3%)
  between operations  14.5 us (2%)
    psum x1, waiting for transfers between devices, per_device(): summed = lax.psum(flat, ('segment', 'rows', 'dp'))  262 us
    dot_general x65, matrix products, product(): return jnp.einsum(form, left, right, preferred_element_type=jnp.float32)  99.6 us
    concatenate x1, local copies, waits for them, and re-layouts, columns(): jnp.concatenate([shifted(values, row_step, col_step, stride) for row_step...  41.8 us
    another operation x11, other arithmetic  18.3 us
    while x128, other arithmetic  17 us
    ppermute x1, waiting for transfers between devices, shifted_2(): return lax.ppermute(block, axis, route)  13.9 us
    all_to_all x1, starting transfers between devices, per_device(): lax.all_to_all(outgoing, 'rows', split_axis=0, concat_axis=0, tiled=True)  13 us
    unnamed x42, local copies, waits for them, and re-layouts  13 us
  transfers between devices with their start and end apart: 5, of which 2 were waited for; matrix products, arithmetic and copies ran while one was open for 20% of the time, Pallas kernels for 0%

profile of v1, /device:TPU:1, one launch (start us, length us, event | category | flops | bytes accessed | tf_op | source)
XLA Modules:
  0.0 621.6 jit_solution(2937329969966064433)
XLA Ops:
  8.2 3.9 collective-permute-start
  14.4 9.0 %reduce-window.6 = s32[32,8,128]{2,1,0:T(8,128)S(1)} reduce-window(s32[32,8,128]{2,1,0:T(8,128)S(1)} %fusion.34, s32[]{:T(128)} %constant.289.clone.1), window={size=1x1x128 pad=0_0x0_0x127_0}, to_apply=%region_2.3 | reduce-window | flops 4161536 | bytes 262148 | tf_op jit(solution)/shard_map/reduce-window
  25.7 2.0 gather_fusion.1
  27.7 3.2 broadcast_select_fusion
  30.9 13.0 %all-to-all-start = ((bf16[32,2,64,144]{3,2,1,0:T(8,128)(2,1)}), bf16[32,2,64,144]{3,2,1,0:T(8,128)(2,1)}, u32[]{:S(2)}, u32[]{:S(2)}) async-start(bf16[32,2,64,144]{3,2,1,0:T(8,128)(2,1)} %broadcast_select_fusion), calls=%async_computation | async-start | bytes 4194304 | tf_op jit(solution)/shard_map/all_to_all | solution.py:216
  46.0 4.3 slice_select_fusion.1
  50.3 41.8 %concatenate.38 = bf16[900,3584]{1,0:T(8,128)(2,1)} concatenate(bf16[100,3584]{1,0:T(8,128)(2,1)} %get-tuple-element.364, bf16[100,3584]{1,0:T(8,128)(2,1)} %get-tuple-element.367, bf16[100,3584]{1,0:T(8,128)(2,1)} %get-tuple-element.357, bf16[100,3584]{1,0:T(8,128)(2,1)} %get-tuple-element.365, bf16[100,3584]{1,0:T(8,128)(2,1)} %get-tuple-element.368, ...), dimensions={0} | concatenate | bytes 12902400 | tf_op jit(solution)/shard_map/concatenate | solution.py:50
  92.2 5.4 fusion.26
  99.4 4.9 pad_maximum_fusion.2
  104.3 4.6 copy.115
  113.4 13.9 %collective-permute-done.2 = bf16[2,64,11,256]{3,1,2,0:T(8,128)(2,1)} collective-permute-done((bf16[2,64,11,256]{3,1,2,0:T(8,128)(2,1)}, bf16[2,64,11,256]{3,1,2,0:T(8,128)(2,1)}, u32[]{:S(2)}, u32[]{:S(2)}) %collective-permute-start.2) | collective-permute-done | bytes 720928 | tf_op jit(solution)/shard_map/ppermute | solution.py:34
  127.3 4.7 copy.116
  131.9 8.6 %pad_maximum_fusion.1 = bf16[2,64,23,256]{1,0,3,2:T(2,128)(2,1)} fusion(bf16[2,64,11,256]{1,0,3,2:T(2,128)(2,1)} %copy.116, bf16[1,64,12,256]{1,0,3,2:T(2,128)(2,1)S(1)} %copy.114, bf16[1,64,12,256]{1,0,3,2:T(2,128)(2,1)} %copy-done.4), kind=kLoop, calls=%fused_computation.86 | loop fusion | flops 4521984 | bytes 3014656 | tf_op jit(solution)/shard_map/concatenate | solution.py:224
  140.5 8.6 %gather_fusion = bf16[32,2,64,12,12]{2,1,4,3,0:T(2,128)(2,1)S(1)} fusion(bf16[2,64,23,256]{1,0,3,2:T(2,128)(2,1)} %pad_maximum_fusion.1, s32[32]{0:T(128)S(1)} %get-tuple-element.375), kind=kCustom, calls=%fused_computation | custom fusion | bytes 2359808 | tf_op jit(solution)/shard_map/vmap()/gather | solution.py:191
  149.2 5.4 fusion.60
  154.5 6.0 copy.139
  160.6 3.4 copy.140
  164.0 2.3 gather_fusion.2
  167.4 176.2 %while.21 = (s32[]{:T(128)}, f32[128,1152]{1,0:T(8,128)S(1)}, f32[128,1152]{1,0:T(8,128)}, f32[64,128]{1,0:T(8,128)S(1)}, f32[32,128]{1,0:T(8,128)S(1)}, /*index...) while((s32[]{:T(128)}, f32[128,1152]{1,0:T(8,128)S(1)}, ...), condition=%wide.region_12.13_spmd.clone, body=%wide.region_6.12_spmd.clone.sunk | while | flops 884677568 | bytes 47296392 | solution.py:162
  198.0 1.9 multiply_reduce_fusion.7
  202.5 2.8 fusion.111
  224.6 2.8 fusion.111
  242.3 1.9 multiply_reduce_fusion.7
  246.7 2.8 fusion.111
  264.4 1.9 multiply_reduce_fusion.7
  268.9 2.8 fusion.111
  291.0 2.8 fusion.111
  308.7 1.9 multiply_reduce_fusion.7
  313.1 2.8 fusion.111
  330.8 1.9 multiply_reduce_fusion.7
  335.2 2.8 fusion.111
  346.4 261.8 %all-reduce.13.cloned.1.call-done = f32[307456]{0:T(1024)} async-done(((f32[307456]{0:T(1024)}), f32[307456]{0:T(1024)}) %all-reduce.13.cloned.1.call-update) | async-done | bytes 1229840 | tf_op jit(solution)/shard_map/psum | solution.py:238
  (601 shorter events, 168.0 us)
Async XLA Ops:
  7.2 18.5 %copy-start = (bf16[1,1,64,64,144]{4,3,2,1,0:T(8,128)(2,1)S(1)}, bf16[1,1,64,64,144]{4,3,2,1,0:T(8,128)(2,1)}, u32[]{:S(2)}) copy-start(bf16[1,1,64,64,144]{4,3,2,1,0:T(8,128)(2,1)} %param.14) | copy-start | bytes 3538948
  8.2 37.2 %collective-permute-start = (bf16[1,100,1,256]{3,1,2,0:T(8,128)(2,1)S(1)}, bf16[1,100,1,256]{3,1,2,0:T(8,128)(2,1)S(1)}, u32[]{:S(2)}, u32[]{:S(2)}) collective-permute-start(bf16[1,100,1,256]{3,1,2,0:T(8,128)(2,1)S(1)} %get-tuple-element.370), channel_id=1, source_target_pairs={{0,4},{4,8},{8,12},{12,16},{16,20},{20,24},{24,28},{28,32},{32,36}... | collective-permute-start | bytes 153608 | tf_op jit(solution)/shard_map/ppermute | solution.py:22
  12.1 33.2 %collective-permute-start.1 = (bf16[1,100,1,256]{3,1,2,0:T(8,128)(2,1)S(1)}, bf16[1,100,1,256]{3,1,2,0:T(8,128)(2,1)S(1)}, u32[]{:S(2)}, u32[]{:S(2)}) collective-permute-start(bf16[1,100,1,256]{3,1,2,0:T(8,128)(2,1)S(1)} %get-tuple-element.371), channel_id=1, source_target_pairs={{4,0},{8,4},{12,8},{16,12},{20,16},{24,20},{28,24},{32,28},{36,32}... | collective-permute-start | bytes 153608 | tf_op jit(solution)/shard_map/ppermute | solution.py:24
  30.9 13.3 %copy-start.15 = (bf16[1,64,12,256]{3,1,2,0:T(8,128)(2,1)S(1)}, bf16[1,64,12,256]{3,1,2,0:T(8,128)(2,1)}, u32[]{:S(2)}) copy-start(bf16[1,64,12,256]{3,1,2,0:T(8,128)(2,1)} %param.13) | copy-start | bytes 1179652
  30.9 14.4 %copy-start.11 = (bf16[1,100,12,256]{3,1,2,0:T(8,128)(2,1)S(1)}, bf16[1,100,12,256]{3,1,2,0:T(8,128)(2,1)}, u32[]{:S(2)}) copy-start(bf16[1,100,12,256]{3,1,2,0:T(8,128)(2,1)} %param.12) | copy-start | bytes 1843204
  30.9 133.1 %all-to-all-start = ((bf16[32,2,64,144]{3,2,1,0:T(8,128)(2,1)}), bf16[32,2,64,144]{3,2,1,0:T(8,128)(2,1)}, u32[]{:S(2)}, u32[]{:S(2)}) async-start(bf16[32,2,64,144]{3,2,1,0:T(8,128)(2,1)} %broadcast_select_fusion), calls=%async_computation | async-start | bytes 4194304 | tf_op jit(solution)/shard_map/all_to_all | solution.py:216
  43.9 564.3 %all-reduce.13.cloned.1.call-start = ((), (), s32[]{:S(2)}) async-start(), calls=%async_computation.1 | async-start | bytes 2465792 | tf_op jit(solution)/shard_map/psum | solution.py:238
  50.3 41.8 %copy-start.24 = (bf16[128,900]{0,1:T(8,128)(2,1)S(1)}, bf16[128,900]{0,1:T(8,128)(2,1)}, u32[]{:S(2)}) copy-start(bf16[128,900]{0,1:T(8,128)(2,1)} %param.16) | copy-start | bytes 691204
  50.3 41.8 %copy-start.25 = (bf16[64,128]{1,0:T(8,128)(2,1)S(1)}, bf16[64,128]{1,0:T(8,128)(2,1)}, u32[]{:S(2)}) copy-start(bf16[64,128]{1,0:T(8,128)(2,1)} %param.17) | copy-start | bytes 49156
  98.3 6.1 copy-start.10
  99.4 11.9 %copy-start.4 = (bf16[1,64,12,256]{1,0,3,2:T(2,128)(2,1)}, bf16[1,64,12,256]{1,0,3,2:T(2,128)(2,1)S(1)}, u32[]{:S(2)}) copy-start(bf16[1,64,12,256]{1,0,3,2:T(2,128)(2,1)S(1)} %copy.113) | copy-start | bytes 1179652
  109.0 18.3 %collective-permute-start.2 = (bf16[2,64,11,256]{3,1,2,0:T(8,128)(2,1)}, bf16[2,64,11,256]{3,1,2,0:T(8,128)(2,1)}, u32[]{:S(2)}, u32[]{:S(2)}) collective-permute-start(bf16[2,64,11,256]{3,1,2,0:T(8,128)(2,1)} %copy.115), channel_id=1, source_target_pairs={{4,0},{8,4},{12,8},{16,12},{20,16},{24,20},{28,24},{32,28},{36,32}... | collective-permute-start | bytes 2162696 | tf_op jit(solution)/shard_map/ppermute | solution.py:34
  154.5 6.0 copy-start.6
  164.0 3.4 copy-start.13
  164.0 3.4 copy-start.22
  168.6 8.4 %copy-start.16 = (f32[4]{0:T(128)}, f32[4]{0:T(128)S(1)}, u32[]{:S(2)}) copy-start(f32[4]{0:T(128)S(1)} %select_reduce_fusion.4) | copy-start | bytes 52 | tf_op jit(solution)/shard_map/while
  175.4 3.5 copy-start.2
  189.6 8.4 %copy-start.16 = (f32[4]{0:T(128)}, f32[4]{0:T(128)S(1)}, u32[]{:S(2)}) copy-start(f32[4]{0:T(128)S(1)} %select_reduce_fusion.4) | copy-start | bytes 52 | tf_op jit(solution)/shard_map/while
  196.5 3.5 copy-start.2
  211.8 8.4 %copy-start.16 = (f32[4]{0:T(128)}, f32[4]{0:T(128)S(1)}, u32[]{:S(2)}) copy-start(f32[4]{0:T(128)S(1)} %select_reduce_fusion.4) | copy-start | bytes 52 | tf_op jit(solution)/shard_map/while
  218.6 3.5 copy-start.2
  233.9 8.4 %copy-start.16 = (f32[4]{0:T(128)}, f32[4]{0:T(128)S(1)}, u32[]{:S(2)}) copy-start(f32[4]{0:T(128)S(1)} %select_reduce_fusion.4) | copy-start | bytes 52 | tf_op jit(solution)/shard_map/while
  240.7 3.5 copy-start.2
  256.0 8.4 %copy-start.16 = (f32[4]{0:T(128)}, f32[4]{0:T(128)S(1)}, u32[]{:S(2)}) copy-start(f32[4]{0:T(128)S(1)} %select_reduce_fusion.4) | copy-start | bytes 52 | tf_op jit(solution)/shard_map/while
  262.9 3.5 copy-start.2
  278.1 8.4 %copy-start.16 = (f32[4]{0:T(128)}, f32[4]{0:T(128)S(1)}, u32[]{:S(2)}) copy-start(f32[4]{0:T(128)S(1)} %select_reduce_fusion.4) | copy-start | bytes 52 | tf_op jit(solution)/shard_map/while
  285.0 3.5 copy-start.2
  300.3 8.4 %copy-start.16 = (f32[4]{0:T(128)}, f32[4]{0:T(128)S(1)}, u32[]{:S(2)}) copy-start(f32[4]{0:T(128)S(1)} %select_reduce_fusion.4) | copy-start | bytes 52 | tf_op jit(solution)/shard_map/while
  307.1 3.5 copy-start.2
  322.4 8.4 %copy-start.16 = (f32[4]{0:T(128)}, f32[4]{0:T(128)S(1)}, u32[]{:S(2)}) copy-start(f32[4]{0:T(128)S(1)} %select_reduce_fusion.4) | copy-start | bytes 52 | tf_op jit(solution)/shard_map/while
  329.2 3.5 copy-start.2
  346.4 268.4 %copy-start.1 = (bf16[1,1,64,64,144]{4,3,2,1,0:T(8,128)(2,1)S(1)}, bf16[1,1,64,64,144]{4,3,2,1,0:T(8,128)(2,1)}, u32[]{:S(2)}) copy-start(bf16[1,1,64,64,144]{4,3,2,1,0:T(8,128)(2,1)} %param.14) | copy-start | bytes 3538948
  (70 other events, 128.7 us)
Sparse Core Ops, SparseCore 0:
  346.5 261.6 all-reduce.12

commit v2 on v1

--- a/solution.py
+++ b/solution.py
@@ -184,6 +184,47 @@
     return jnp.sum(hits * owner_slot[:, :, None], axis=1)
 
 
+def exchange_sum(flat, steps):
+    spread = 1
+    for _, distance in steps:
+        spread *= 2
+    size = flat.shape[0]
+    unit = spread * 8
+    padded = (size + unit - 1) // unit * unit
+    values = jnp.pad(flat, (0, padded - size))
+    places = {axis: lax.axis_index(axis) for axis, _ in steps}
+    for axis, distance in steps:
+        count = lax.axis_size(axis)
+        half = values.shape[0] // 2
+        low, high = values[:half], values[half:]
+        upper = (places[axis] // distance) % 2 == 1
+        route = [(i, i ^ distance) for i in range(count)]
+        kept = jnp.where(upper, high, low)
+        sent = jnp.where(upper, low, high)
+        values = kept + lax.ppermute(sent, axis, route)
+    for axis, distance in reversed(steps):
+        count = lax.axis_size(axis)
+        upper = (places[axis] // distance) % 2 == 1
+        route = [(i, i ^ distance) for i in range(count)]
+        other = lax.ppermute(values, axis, route)
+        values = jnp.where(
+            upper, jnp.concatenate([other, values]), jnp.concatenate([values, other])
+        )
+    return values[:size]
+
+
+def reduce_steps():
+    sizes = {axis: lax.axis_size(axis) for axis in ("segment", "rows", "dp")}
+    steps = []
+    distance = 1
+    while distance < max(sizes.values()):
+        for axis in ("segment", "rows", "dp"):
+            if distance < sizes[axis]:
+                steps.append((axis, distance))
+        distance *= 2
+    return steps
+
+
 def cut_patches(source_grid, row_at, col_at, height):
     zero_index = jnp.zeros((), jnp.int32)
 
@@ -235,7 +276,7 @@
     owner_table = sample_hot[:, None] * owner_part[None, :]
     pieces = (gradients[0], gradients[1], gradients[2], gradients[3], owner_table)
     flat = jnp.concatenate([piece.reshape(-1) for piece in pieces])
-    summed = lax.psum(flat, ("segment", "rows", "dp"))
+    summed = exchange_sum(flat, reduce_steps())
     results = []
     offset = 0
     for piece in pieces:

time: 627 us -> 453 us (0.72)
  waiting for transfers between devices: 276 us -> 47 us
  starting transfers between devices: 20 us -> 74.4 us
  between operations: 14.5 us -> 5.14 us
  other arithmetic: 81.4 us -> 87.9 us
    psum x1 -> x0, waiting for transfers between devices: 262 us -> none  [per_device(): summed = lax.psum(flat, ('segment', 'rows', 'dp'))]
    ppermute x0 -> x16, starting transfers between devices: none -> 54.1 us  [the longest x8 31.3 us: exchange_sum(): other = lax.ppermute(values, axis, route)]
    ppermute x0 -> x16, waiting for transfers between devices: none -> 33.3 us  [the longest x8 19.4 us: exchange_sum(): values = kept + lax.ppermute(sent, axis, route)]
    unnamed x42 -> x40, local copies, waits for them, and re-layouts: 13 us -> 11.9 us
  transfers between devices with their start and end apart: 5 -> 20, of which waited for: 2 -> 16; matrix products, arithmetic and copies ran while one was open for 20% -> 29% of each run, Pallas kernels for 0% -> 0%
where the time goes in v2:
time: 453 us; the launch traced here: 446 us
  local copies, waits for them, and re-layouts  130 us (29%)
  matrix products  98.7 us (22%)
  other arithmetic  87.9 us (19%)
  starting transfers between devices  74.4 us (16%)
  waiting for transfers between devices  47 us (10%)
  between operations  5.14 us (1%)
    dot_general x65, matrix products, product(): return jnp.einsum(form, left, right, preferred_element_type=jnp.float32)  98.7 us
    concatenate x1, local copies, waits for them, and re-layouts, columns(): jnp.concatenate([shifted(values, row_step, col_step, stride) for row_step...  41.9 us
    ppermute x8, starting transfers between devices, exchange_sum(): other = lax.ppermute(values, axis, route)  31.3 us
    ppermute x8, starting transfers between devices, exchange_sum(): values = kept + lax.ppermute(sent, axis, route)  22.8 us
    ppermute x8, waiting for transfers between devices, exchange_sum(): values = kept + lax.ppermute(sent, axis, route)  19.4 us
    another operation x11, other arithmetic  18.3 us
    while x128, other arithmetic  17 us
    ppermute x8, waiting for transfers between devices, exchange_sum(): other = lax.ppermute(values, axis, route)  13.9 us
  transfers between devices with their start and end apart: 20, of which 16 were waited for; matrix products, arithmetic and copies ran while one was open for 29% of the time, Pallas kernels for 0%

profile of v2, /device:TPU:1, one launch (start us, length us, event | category | flops | bytes accessed | tf_op | source)
XLA Modules:
  0.0 446.4 jit_solution(137468169987304410)
XLA Ops:
  1.6 3.9 collective-permute-start
  9.0 9.0 %reduce-window.6 = s32[32,8,128]{2,1,0:T(8,128)S(1)} reduce-window(s32[32,8,128]{2,1,0:T(8,128)S(1)} %fusion.35, s32[]{:T(128)} %constant.425.clone.1), window={size=1x1x128 pad=0_0x0_0x127_0}, to_apply=%region_2.3 | reduce-window | flops 4161536 | bytes 262148 | tf_op jit(solution)/shard_map/reduce-window
  21.2 3.2 broadcast_select_fusion
  24.4 13.3 %all-to-all-start = ((bf16[32,2,64,144]{3,2,1,0:T(8,128)(2,1)}), bf16[32,2,64,144]{3,2,1,0:T(8,128)(2,1)}, u32[]{:S(2)}, u32[]{:S(2)}) async-start(bf16[32,2,64,144]{3,2,1,0:T(8,128)(2,1)} %broadcast_select_fusion), calls=%async_computation | async-start | bytes 4194304 | tf_op jit(solution)/shard_map/all_to_all | solution.py:257
  39.6 4.4 slice_select_fusion.1
  44.0 41.9 %concatenate.159 = bf16[900,3584]{1,0:T(8,128)(2,1)} concatenate(bf16[100,3584]{1,0:T(8,128)(2,1)} %get-tuple-element.388, bf16[100,3584]{1,0:T(8,128)(2,1)} %get-tuple-element.391, bf16[100,3584]{1,0:T(8,128)(2,1)} %get-tuple-element.381, bf16[100,3584]{1,0:T(8,128)(2,1)} %get-tuple-element.389, bf16[100,3584]{1,0:T(8,128)(2,1)} %get-tuple-element.392, ...), dimensions={0} | concatenate | bytes 12902400 | tf_op jit(solution)/shard_map/concatenate | solution.py:50
  85.8 5.4 %fusion.26 = bf16[64,3584]{1,0:T(8,128)(2,1)S(1)} fusion(bf16[64,128]{1,0:T(8,128)(2,1)S(1)} %copy-done.24, bf16[900,3584]{1,0:T(8,128)(2,1)} %concatenate.159, bf16[128,900]{0,1:T(8,128)(2,1)S(1)} %copy-done.23), kind=kOutput, calls=%fused_computation.85 | convolution fusion | flops 886996992 | bytes 7156736 | tf_op jit(solution)/shard_map/co,op->cp/dot_general | solution.py:75
  93.1 4.9 %pad_maximum_fusion.2 = bf16[2,64,11,256]{1,0,3,2:T(2,128)(2,1)} fusion(bf16[1,64,12,256]{1,0,3,2:T(2,128)(2,1)S(1)} %copy.147, bf16[1,64,12,256]{1,0,3,2:T(2,128)(2,1)S(1)} %copy.146), kind=kLoop, calls=%fused_computation.89 | loop fusion | flops 1441792 | bytes 1507328 | tf_op jit(solution)/shard_map/stack | solution.py:261
  98.0 4.6 %copy.148 = bf16[2,64,11,256]{3,1,2,0:T(8,128)(2,1)} copy(bf16[2,64,11,256]{1,0,3,2:T(2,128)(2,1)} %pad_maximum_fusion.2) | data formatting | bytes 1441792 | tf_op jit(solution)/shard_map/slice | solution.py:264
  107.2 13.7 %collective-permute-done.2 = bf16[2,64,11,256]{3,1,2,0:T(8,128)(2,1)} collective-permute-done((bf16[2,64,11,256]{3,1,2,0:T(8,128)(2,1)}, bf16[2,64,11,256]{3,1,2,0:T(8,128)(2,1)}, u32[]{:S(2)}, u32[]{:S(2)}) %collective-permute-start.2) | collective-permute-done | bytes 720928 | tf_op jit(solution)/shard_map/ppermute | solution.py:34
  120.9 4.7 %copy.149 = bf16[2,64,11,256]{1,0,3,2:T(2,128)(2,1)} copy(bf16[2,64,11,256]{3,1,2,0:T(8,128)(2,1)} %collective-permute-done.2) | data formatting | bytes 1441792 | tf_op jit(solution)/shard_map/ppermute | solution.py:34
  125.5 8.5 %pad_maximum_fusion.1 = bf16[2,64,23,256]{1,0,3,2:T(2,128)(2,1)} fusion(bf16[2,64,11,256]{1,0,3,2:T(2,128)(2,1)} %copy.149, bf16[1,64,12,256]{1,0,3,2:T(2,128)(2,1)S(1)} %copy.147, bf16[1,64,12,256]{1,0,3,2:T(2,128)(2,1)} %copy-done.4), kind=kLoop, calls=%fused_computation.86 | loop fusion | flops 4521984 | bytes 3014656 | tf_op jit(solution)/shard_map/concatenate | solution.py:265
  134.1 8.6 %gather_fusion = bf16[32,2,64,12,12]{2,1,4,3,0:T(2,128)(2,1)S(1)} fusion(bf16[2,64,23,256]{1,0,3,2:T(2,128)(2,1)} %pad_maximum_fusion.1, s32[32]{0:T(128)S(1)} %get-tuple-element.403), kind=kCustom, calls=%fused_computation | custom fusion | bytes 2359808 | tf_op jit(solution)/shard_map/vmap()/gather | solution.py:232
  142.7 5.4 %fusion.61 = (bf16[32,1,64,144]{2,1,3,0:T(2,128)(2,1)}, bf16[32,1,64,144]{2,1,3,0:T(2,128)(2,1)}) fusion(bf16[32,2,64,144]{2,1,3,0:T(2,128)(2,1)S(1)} %bitcast.212), kind=kLoop, calls=%fused_computation.208 | loop fusion | bytes 2359296 | tf_op jit(solution)/shard_map/slice | solution.py:271
  148.1 6.0 %copy.183 = bf16[32,1,64,144]{3,2,0,1:T(8,128)(2,1)} copy(bf16[32,1,64,144]{2,1,3,0:T(2,128)(2,1)} %get-tuple-element.376) | data formatting | bytes 1179648
  154.2 3.4 copy.184
  161.0 174.7 %while.21 = (s32[]{:T(128)}, f32[128,1152]{1,0:T(8,128)S(1)}, f32[128,1152]{1,0:T(8,128)}, f32[64,128]{1,0:T(8,128)S(1)}, f32[32,128]{1,0:T(8,128)S(1)}, /*index...) while((s32[]{:T(128)}, f32[128,1152]{1,0:T(8,128)S(1)}, ...), condition=%wide.region_12.13_spmd.clone, body=%wide.region_6.12_spmd.clone.sunk | while | flops 884677568 | bytes 47296392 | solution.py:162
  195.6 2.8 fusion.112
  217.5 2.8 fusion.112
  239.5 2.8 fusion.112
  327.3 2.8 fusion.112
  344.4 7.2 %collective-permute-done.4 = f32[77312]{0:T(1024)S(1)} collective-permute-done((f32[77312]{0:T(1024)S(1)}, f32[77312]{0:T(1024)S(1)}, u32[]{:S(2)}, u32[]{:S(2)}) %collective-permute-start.4) | collective-permute-done | bytes 309280 | tf_op jit(solution)/shard_map/ppermute | solution.py:204
  355.9 5.4 %collective-permute-start.6 = (f32[19328]{0:T(1024)S(1)}, f32[19328]{0:T(1024)S(1)}, u32[]{:S(2)}, u32[]{:S(2)}) collective-permute-start(f32[19328]{0:T(1024)S(1)} %slice_select_fusion.11), channel_id=1, source_target_pairs={{0,8},{4,12},{8,0},{12,4},{16,24},{20,28},{24,16},{28,20},{32,40},... | collective-permute-start | bytes 231944 | tf_op jit(solution)/shard_map/ppermute | solution.py:204
  363.2 3.0 collective-permute-start.7
  370.9 2.9 collective-permute-start.9
  375.1 4.9 %collective-permute-start.10 = (f32[1208]{0:T(1024)S(1)}, f32[1208]{0:T(1024)S(1)}, u32[]{:S(2)}, u32[]{:S(2)}) collective-permute-start(f32[1208]{0:T(1024)S(1)} %slice_select_fusion.15), channel_id=1, source_target_pairs={{0,64},{4,68},{8,72},{12,76},{16,80},{20,84},{24,88},{28,92},{32,9... | collective-permute-start | bytes 14504 | tf_op jit(solution)/shard_map/ppermute | solution.py:204
  381.6 4.9 %collective-permute-start.11 = (f32[1208]{0:T(1024)S(1)}, f32[1208]{0:T(1024)S(1)}, u32[]{:S(2)}, u32[]{:S(2)}) collective-permute-start(f32[1208]{0:T(1024)S(1)} %select_add_fusion.8), channel_id=1, source_target_pairs={{0,64},{4,68},{8,72},{12,76},{16,80},{20,84},{24,88},{28,92},{32,9... | collective-permute-start | bytes 14504 | tf_op jit(solution)/shard_map/ppermute | solution.py:209
  395.1 3.0 collective-permute-start.14
  399.7 3.3 collective-permute-start.15
  406.4 2.8 collective-permute-done.16
  411.4 4.0 collective-permute-done.17
  415.5 14.5 %collective-permute-start.18 = (f32[154624]{0:T(1024)S(1)}, f32[154624]{0:T(1024)S(1)}, u32[]{:S(2)}, u32[]{:S(2)}) collective-permute-start(f32[154624]{0:T(1024)S(1)} %maximum_select_fusion.3), channel_id=1, source_target_pairs={{0,128},{128,0},{1,129},{129,1},{2,130},{130,2},{3,131},{131,3},{4... | collective-permute-start | bytes 1855496 | tf_op jit(solution)/shard_map/ppermute | solution.py:209
  (667 shorter events, 230.2 us)
Async XLA Ops:
  0.6 18.5 %copy-start = (bf16[1,1,64,64,144]{4,3,2,1,0:T(8,128)(2,1)S(1)}, bf16[1,1,64,64,144]{4,3,2,1,0:T(8,128)(2,1)}, u32[]{:S(2)}) copy-start(bf16[1,1,64,64,144]{4,3,2,1,0:T(8,128)(2,1)} %param.14) | copy-start | bytes 3538948
  1.6 37.3 %collective-permute-start = (bf16[1,100,1,256]{3,1,2,0:T(8,128)(2,1)S(1)}, bf16[1,100,1,256]{3,1,2,0:T(8,128)(2,1)S(1)}, u32[]{:S(2)}, u32[]{:S(2)}) collective-permute-start(bf16[1,100,1,256]{3,1,2,0:T(8,128)(2,1)S(1)} %get-tuple-element.394), channel_id=1, source_target_pairs={{0,4},{4,8},{8,12},{12,16},{16,20},{20,24},{24,28},{28,32},{32,36}... | collective-permute-start | bytes 153608 | tf_op jit(solution)/shard_map/ppermute | solution.py:22
  5.6 33.3 %collective-permute-start.1 = (bf16[1,100,1,256]{3,1,2,0:T(8,128)(2,1)S(1)}, bf16[1,100,1,256]{3,1,2,0:T(8,128)(2,1)S(1)}, u32[]{:S(2)}, u32[]{:S(2)}) collective-permute-start(bf16[1,100,1,256]{3,1,2,0:T(8,128)(2,1)S(1)} %get-tuple-element.395), channel_id=1, source_target_pairs={{4,0},{8,4},{12,8},{16,12},{20,16},{24,20},{28,24},{32,28},{36,32}... | collective-permute-start | bytes 153608 | tf_op jit(solution)/shard_map/ppermute | solution.py:24
  24.4 13.4 %copy-start.14 = (bf16[1,64,12,256]{3,1,2,0:T(8,128)(2,1)S(1)}, bf16[1,64,12,256]{3,1,2,0:T(8,128)(2,1)}, u32[]{:S(2)}) copy-start(bf16[1,64,12,256]{3,1,2,0:T(8,128)(2,1)} %param.13) | copy-start | bytes 1179652
  24.4 14.5 %copy-start.10 = (bf16[1,100,12,256]{3,1,2,0:T(8,128)(2,1)S(1)}, bf16[1,100,12,256]{3,1,2,0:T(8,128)(2,1)}, u32[]{:S(2)}) copy-start(bf16[1,100,12,256]{3,1,2,0:T(8,128)(2,1)} %param.12) | copy-start | bytes 1843204
  24.4 133.2 %all-to-all-start = ((bf16[32,2,64,144]{3,2,1,0:T(8,128)(2,1)}), bf16[32,2,64,144]{3,2,1,0:T(8,128)(2,1)}, u32[]{:S(2)}, u32[]{:S(2)}) async-start(bf16[32,2,64,144]{3,2,1,0:T(8,128)(2,1)} %broadcast_select_fusion), calls=%async_computation | async-start | bytes 4194304 | tf_op jit(solution)/shard_map/all_to_all | solution.py:257
  44.0 41.9 %copy-start.23 = (bf16[128,900]{0,1:T(8,128)(2,1)S(1)}, bf16[128,900]{0,1:T(8,128)(2,1)}, u32[]{:S(2)}) copy-start(bf16[128,900]{0,1:T(8,128)(2,1)} %param.16) | copy-start | bytes 691204
  44.0 41.9 %copy-start.24 = (bf16[64,128]{1,0:T(8,128)(2,1)S(1)}, bf16[64,128]{1,0:T(8,128)(2,1)}, u32[]{:S(2)}) copy-start(bf16[64,128]{1,0:T(8,128)(2,1)} %param.17) | copy-start | bytes 49156
  93.1 12.2 %copy-start.4 = (bf16[1,64,12,256]{1,0,3,2:T(2,128)(2,1)}, bf16[1,64,12,256]{1,0,3,2:T(2,128)(2,1)S(1)}, u32[]{:S(2)}) copy-start(bf16[1,64,12,256]{1,0,3,2:T(2,128)(2,1)S(1)} %copy.146) | copy-start | bytes 1179652
  102.6 18.3 %collective-permute-start.2 = (bf16[2,64,11,256]{3,1,2,0:T(8,128)(2,1)}, bf16[2,64,11,256]{3,1,2,0:T(8,128)(2,1)}, u32[]{:S(2)}, u32[]{:S(2)}) collective-permute-start(bf16[2,64,11,256]{3,1,2,0:T(8,128)(2,1)} %copy.148), channel_id=1, source_target_pairs={{4,0},{8,4},{12,8},{16,12},{20,16},{24,20},{28,24},{32,28},{36,32}... | collective-permute-start | bytes 2162696 | tf_op jit(solution)/shard_map/ppermute | solution.py:34
  204.9 8.3 %copy-start.15 = (f32[4]{0:T(128)}, f32[4]{0:T(128)S(1)}, u32[]{:S(2)}) copy-start(f32[4]{0:T(128)S(1)} %select_reduce_fusion.4) | copy-start | bytes 52 | tf_op jit(solution)/shard_map/while
  226.8 8.3 %copy-start.15 = (f32[4]{0:T(128)}, f32[4]{0:T(128)S(1)}, u32[]{:S(2)}) copy-start(f32[4]{0:T(128)S(1)} %select_reduce_fusion.4) | copy-start | bytes 52 | tf_op jit(solution)/shard_map/while
  248.8 8.3 %copy-start.15 = (f32[4]{0:T(128)}, f32[4]{0:T(128)S(1)}, u32[]{:S(2)}) copy-start(f32[4]{0:T(128)S(1)} %select_reduce_fusion.4) | copy-start | bytes 52 | tf_op jit(solution)/shard_map/while
  270.7 8.3 %copy-start.15 = (f32[4]{0:T(128)}, f32[4]{0:T(128)S(1)}, u32[]{:S(2)}) copy-start(f32[4]{0:T(128)S(1)} %select_reduce_fusion.4) | copy-start | bytes 52 | tf_op jit(solution)/shard_map/while
  292.7 8.3 %copy-start.15 = (f32[4]{0:T(128)}, f32[4]{0:T(128)S(1)}, u32[]{:S(2)}) copy-start(f32[4]{0:T(128)S(1)} %select_reduce_fusion.4) | copy-start | bytes 52 | tf_op jit(solution)/shard_map/while
  314.6 8.3 %copy-start.15 = (f32[4]{0:T(128)}, f32[4]{0:T(128)S(1)}, u32[]{:S(2)}) copy-start(f32[4]{0:T(128)S(1)} %select_reduce_fusion.4) | copy-start | bytes 52 | tf_op jit(solution)/shard_map/while
  337.4 4.3 collective-permute-start.3
  343.0 8.7 %collective-permute-start.4 = (f32[77312]{0:T(1024)S(1)}, f32[77312]{0:T(1024)S(1)}, u32[]{:S(2)}, u32[]{:S(2)}) collective-permute-start(f32[77312]{0:T(1024)S(1)} %slice_select_fusion.9), channel_id=1, source_target_pairs={{0,4},{4,0},{8,12},{12,8},{16,20},{20,16},{24,28},{28,24},{32,36},... | collective-permute-start | bytes 927752 | tf_op jit(solution)/shard_map/ppermute | solution.py:204
  351.7 4.2 collective-permute-start.5
  355.9 7.2 %collective-permute-start.6 = (f32[19328]{0:T(1024)S(1)}, f32[19328]{0:T(1024)S(1)}, u32[]{:S(2)}, u32[]{:S(2)}) collective-permute-start(f32[19328]{0:T(1024)S(1)} %slice_select_fusion.11), channel_id=1, source_target_pairs={{0,8},{4,12},{8,0},{12,4},{16,24},{20,28},{24,16},{28,20},{32,40},... | collective-permute-start | bytes 231944 | tf_op jit(solution)/shard_map/ppermute | solution.py:204
  363.2 4.4 collective-permute-start.7
  367.8 3.0 collective-permute-start.8
  370.9 4.0 collective-permute-start.9
  375.1 6.4 %collective-permute-start.10 = (f32[1208]{0:T(1024)S(1)}, f32[1208]{0:T(1024)S(1)}, u32[]{:S(2)}, u32[]{:S(2)}) collective-permute-start(f32[1208]{0:T(1024)S(1)} %slice_select_fusion.15), channel_id=1, source_target_pairs={{0,64},{4,68},{8,72},{12,76},{16,80},{20,84},{24,88},{28,92},{32,9... | collective-permute-start | bytes 14504 | tf_op jit(solution)/shard_map/ppermute | solution.py:204
  381.6 6.4 %collective-permute-start.11 = (f32[1208]{0:T(1024)S(1)}, f32[1208]{0:T(1024)S(1)}, u32[]{:S(2)}, u32[]{:S(2)}) collective-permute-start(f32[1208]{0:T(1024)S(1)} %select_add_fusion.8), channel_id=1, source_target_pairs={{0,64},{4,68},{8,72},{12,76},{16,80},{20,84},{24,88},{28,92},{32,9... | collective-permute-start | bytes 14504 | tf_op jit(solution)/shard_map/ppermute | solution.py:209
  388.1 3.6 collective-permute-start.12
  391.8 3.3 collective-permute-start.13
  395.1 4.4 collective-permute-start.14
  399.7 5.0 %collective-permute-start.15 = (f32[19328]{0:T(1024)S(1)}, f32[19328]{0:T(1024)S(1)}, u32[]{:S(2)}, u32[]{:S(2)}) collective-permute-start(f32[19328]{0:T(1024)S(1)} %maximum_select_fusion.11), channel_id=1, source_target_pairs={{0,8},{4,12},{8,0},{12,4},{16,24},{20,28},{24,16},{28,20},{32,40},... | collective-permute-start | bytes 231944 | tf_op jit(solution)/shard_map/ppermute | solution.py:209
  404.7 4.5 collective-permute-start.16
  409.3 6.1 %collective-permute-start.17 = (f32[77312]{0:T(1024)S(1)}, f32[77312]{0:T(1024)S(1)}, u32[]{:S(2)}, u32[]{:S(2)}) collective-permute-start(f32[77312]{0:T(1024)S(1)} %maximum_select_fusion.5), channel_id=1, source_target_pairs={{0,4},{4,0},{8,12},{12,8},{16,20},{20,16},{24,28},{28,24},{32,36},... | collective-permute-start | bytes 927752 | tf_op jit(solution)/shard_map/ppermute | solution.py:209
  415.5 18.4 %collective-permute-start.18 = (f32[154624]{0:T(1024)S(1)}, f32[154624]{0:T(1024)S(1)}, u32[]{:S(2)}, u32[]{:S(2)}) collective-permute-start(f32[154624]{0:T(1024)S(1)} %maximum_select_fusion.3), channel_id=1, source_target_pairs={{0,128},{128,0},{1,129},{129,1},{2,130},{130,2},{3,131},{131,3},{4... | collective-permute-start | bytes 1855496 | tf_op jit(solution)/shard_map/ppermute | solution.py:209
  (83 other events, 194.5 us)

commit v3 on v2

--- a/solution.py
+++ b/solution.py
@@ -3,6 +3,8 @@
 import jax
 import jax.numpy as jnp
 from jax import lax
+from jax.experimental import pallas as pl
+from jax.experimental.pallas import tpu as pltpu
 from jax.sharding import PartitionSpec as P
 
 PATCH = 12
@@ -163,6 +165,160 @@
     return (losses.reshape(patch_count), gradients)
 
 
+def tap_masks(rows):
+    cell = jnp.arange(rows, dtype=jnp.int32) % (PATCH * PATCH)
+    line = cell // PATCH
+    place = cell % PATCH
+    cols = []
+    for row_step, col_step in TAPS:
+        inside = (line + row_step >= 0) & (line + row_step < PATCH)
+        inside = inside & (place + col_step >= 0) & (place + col_step < PATCH)
+        cols.append(inside.astype(jnp.float32))
+    cols += [jnp.zeros((rows,), jnp.float32)] * (16 - len(cols))
+    return jnp.stack(cols, axis=1)
+
+
+def sig(values):
+    return 1.0 / (1.0 + jnp.exp(-values))
+
+
+def patch_kernel(xin_ref, skip_ref, scale_ref, emb_ref, mask_ref, w1t_ref, w2t_ref, w2_ref,
+                 pt_ref, pm_ref, err_ref, sums_ref, g1_ref, g2_ref, gp_ref, cin_ref, cone_ref):
+    rows = xin_ref.shape[0]
+    groups = sums_ref.shape[0]
+    cells = rows // groups
+    channels = xin_ref.shape[1]
+
+    @pl.when(pl.program_id(0) == 0)
+    def _():
+        g1_ref[...] = jnp.zeros_like(g1_ref)
+        g2_ref[...] = jnp.zeros_like(g2_ref)
+        gp_ref[...] = jnp.zeros_like(gp_ref)
+
+    def stack(values, target):
+        for tap, (row_step, col_step) in enumerate(TAPS):
+            shift = row_step * PATCH + col_step
+            moved = values if shift == 0 else pltpu.roll(values, (-shift) % rows, 0)
+            moved = moved * mask_ref[:, tap : tap + 1]
+            target[:, tap * channels : (tap + 1) * channels] = moved.astype(target.dtype)
+
+    stack(xin_ref[...].astype(jnp.float32), cin_ref)
+    pre_one = jnp.dot(cin_ref[...], w1t_ref[...], preferred_element_type=jnp.float32)
+    pre_one = pre_one + emb_ref[...]
+    gate_one = sig(pre_one)
+    act_one = (pre_one * gate_one).astype(jnp.bfloat16)
+    stack(act_one.astype(jnp.float32), cone_ref)
+    pre_two = jnp.dot(cone_ref[...], w2t_ref[...], preferred_element_type=jnp.float32)
+    gate_two = sig(pre_two)
+    act_two = (pre_two * gate_two).astype(jnp.bfloat16)
+    output = jnp.dot(act_two, pt_ref[...], preferred_element_type=jnp.float32)
+    error = skip_ref[...] + scale_ref[:, 0:1] * output
+    err_ref[...] = error
+    grad_output = (scale_ref[:, 1:2] * error).astype(jnp.bfloat16)
+    contract = (((0,), (0,)), ((), ()))
+    gp_ref[...] += lax.dot_general(grad_output, act_two, contract, preferred_element_type=jnp.float32)
+    grad_act_two = jnp.dot(grad_output, pm_ref[...], preferred_element_type=jnp.float32)
+    slope_two = gate_two * (1.0 + pre_two * (1.0 - gate_two))
+    grad_pre_two = (grad_act_two * slope_two).astype(jnp.bfloat16)
+    g2_ref[...] += lax.dot_general(grad_pre_two, cone_ref[...], contract, preferred_element_type=jnp.float32)
+    grad_act_one = jnp.zeros((rows, channels), jnp.float32)
+    for tap, (row_step, col_step) in enumerate(TAPS):
+        shift = row_step * PATCH + col_step
+        piece = jnp.dot(grad_pre_two, w2_ref[:, tap * channels : (tap + 1) * channels],
+                        preferred_element_type=jnp.float32)
+        moved = piece if shift == 0 else pltpu.roll(piece, shift % rows, 0)
+        grad_act_one = grad_act_one + moved * mask_ref[:, 8 - tap : 9 - tap]
+    slope_one = gate_one * (1.0 + pre_one * (1.0 - gate_one))
+    grad_pre_one = (grad_act_one * slope_one).astype(jnp.bfloat16)
+    g1_ref[...] += lax.dot_general(grad_pre_one, cin_ref[...], contract, preferred_element_type=jnp.float32)
+    wide = grad_pre_one.astype(jnp.float32)
+    for group in range(groups):
+        sums_ref[group : group + 1, :] = jnp.sum(wide[group * cells : (group + 1) * cells], axis=0, keepdims=True)
+
+
+def patch_pass(xin, skip, scale, emb, conv_one, conv_two, out_proj, group=8, interpret=False):
+    rows_all, channels = xin.shape
+    cells = PATCH * PATCH
+    patches = rows_all // cells
+    rows = group * cells
+    steps = patches // group
+    width = conv_one.shape[1]
+    outs = conv_one.shape[0]
+    targets = out_proj.shape[0]
+    masks = tap_masks(rows)
+    block = lambda shape: pl.BlockSpec(shape, lambda i: (i, 0))
+    whole = lambda shape: pl.BlockSpec(shape, lambda i: (0, 0))
+    return pl.pallas_call(
+        patch_kernel,
+        grid=(steps,),
+        in_specs=[
+            block((rows, channels)),
+            block((rows, targets)),
+            block((rows, 8)),
+            block((rows, outs)),
+            whole((rows, 16)),
+            whole((width, outs)),
+            whole((width, outs)),
+            whole((outs, width)),
+            whole((outs, targets)),
+            whole((targets, outs)),
+        ],
+        out_specs=[
+            block((rows, targets)),
+            block((group, outs)),
+            whole((outs, width)),
+            whole((outs, width)),
+            whole((targets, outs)),
+        ],
+        out_shape=[
+            jax.ShapeDtypeStruct((rows_all, targets), jnp.float32),
+            jax.ShapeDtypeStruct((patches, outs), jnp.float32),
+            jax.ShapeDtypeStruct((outs, width), jnp.float32),
+            jax.ShapeDtypeStruct((outs, width), jnp.float32),
+            jax.ShapeDtypeStruct((targets, outs), jnp.float32),
+        ],
+        scratch_shapes=[pltpu.VMEM((rows, width), jnp.bfloat16), pltpu.VMEM((rows, width), jnp.bfloat16)],
+        compiler_params=pltpu.CompilerParams(dimension_semantics=("arbitrary",)),
+        interpret=interpret,
+    )(xin, skip, scale, emb, masks, conv_one.T, conv_two.T, conv_two, out_proj.T, out_proj)
+
+
+def kernel_blocks(mean_part, target_part, noise_part, step_ids, in_use, weights, interpret=False):
+    conv_one, conv_two, out_proj, step_embed = weights
+    patch_count, targets, cells = mean_part.shape
+    level_count = step_embed.shape[0]
+    sigma_table = noise_levels(level_count)
+    step_hot = (step_ids[:, None] == jnp.arange(level_count, dtype=jnp.int32)[None, :]).astype(
+        jnp.float32
+    )
+    sigma = jnp.sum(step_hot * sigma_table[None, :], axis=1)
+    sigma_sq = sigma * sigma + 1.0
+    scale_in = (1.0 / jnp.sqrt(sigma_sq))[:, None, None]
+    scale_skip = (1.0 / sigma_sq)[:, None, None]
+    scale_out = sigma / jnp.sqrt(sigma_sq)
+    weight_loss = sigma_sq / (sigma * sigma)
+    mean_float = mean_part.astype(jnp.float32)
+    residual = target_part.astype(jnp.float32) - mean_float
+    noisy = residual + sigma[:, None, None] * noise_part.astype(jnp.float32)
+    inputs = jnp.concatenate([scale_in * noisy, mean_float], axis=1).astype(jnp.bfloat16)
+    xin = jnp.swapaxes(inputs, 1, 2).reshape(patch_count * cells, 2 * targets)
+    skip = jnp.swapaxes(scale_skip * noisy - residual, 1, 2).reshape(patch_count * cells, targets)
+    factor = 2.0 * weight_loss * in_use / (targets * cells)
+    per_patch = jnp.stack([scale_out, factor * scale_out], axis=1)
+    per_patch = jnp.pad(per_patch, ((0, 0), (0, 6)))
+    scale = jnp.broadcast_to(per_patch[:, None, :], (patch_count, cells, 8)).reshape(-1, 8)
+    embedded = jnp.sum(step_hot[:, :, None] * step_embed[None, :, :], axis=1)
+    emb = jnp.broadcast_to(embedded[:, None, :], (patch_count, cells, embedded.shape[1]))
+    emb = emb.reshape(patch_count * cells, embedded.shape[1])
+    error, pixel_sums, grad_one, grad_two, grad_proj = patch_pass(
+        xin, skip, scale, emb, conv_one, conv_two, out_proj, interpret=interpret
+    )
+    error = error.reshape(patch_count, cells * targets)
+    losses = weight_loss * jnp.mean(error * error, axis=1) * in_use
+    grad_table = jnp.sum(step_hot[:, :, None] * pixel_sums[:, None, :], axis=0)
+    return (losses, (grad_one, grad_two, grad_proj, grad_table))
+
+
 def owner_tables(region_rows, strips):
     owners = region_rows[:, :, 2]
     owner_hot = (owners[:, :, None] == jnp.arange(strips, dtype=jnp.int32)[None, None, :]).astype(
@@ -267,7 +423,7 @@
     flat_recv = received.reshape((strips * capacity,) + received.shape[2:])
     patch_noise = jnp.take(flat_recv, own_regions[:, 2] * capacity + own_pairs, axis=0)
     in_use = jnp.ones((per_strip,), jnp.float32)
-    losses, gradients = run_blocks(
+    losses, gradients = kernel_blocks(
         patches[:, 0], patches[:, 1], patch_noise, own_regions[:, 3], in_use, weights
     )
     owner_hot = (own_regions[:, 2][:, None] == jnp.arange(strips, dtype=jnp.int32)[None, :])

time: 453 us -> 326 us (0.72)
  matrix products: 98.7 us -> 5.4 us
  other arithmetic: 87.9 us -> 50.2 us
  Pallas kernels: 0 us -> 28.8 us
  local copies, waits for them, and re-layouts: 130 us -> 113 us
    dot_general x65 -> x1, matrix products: 98.7 us -> 5.4 us  [product(): return jnp.einsum(form, left, right, preferred_element_type=jnp.float32)]
    pallas_call x0 -> x1, Pallas kernels: none -> 28.8 us  [patch_pass(): pl.pallas_call(patch_kernel, grid=(steps,), in_specs=[block((rows, channe...]
    while x128 -> x0, other arithmetic: 17 us -> none
    dynamic_update_slice x8 -> x0, local copies, waits for them, and re-layouts: 10.4 us -> none  [run_blocks(): gradients, losses = lax.scan(advance, initial, stacked)]
    reduce_sum x32 -> x5, other arithmetic: 12.8 us -> 3.05 us  [the longest x2 2.46 us: kernel_blocks(): losses = weight_loss * jnp.mean(error * error, axis=1) * in_use]
    another operation x11 -> x4, other arithmetic: 18.3 us -> 9.16 us
    convert_element_type x8 -> x0, local copies, waits for them, and re-layouts: 7.36 us -> none  [patch_block(): mean_float = mean_part.astype(jnp.float32)]
    transpose x0 -> x2, local copies, waits for them, and re-layouts: none -> 5.89 us  [the longest x1 3.77 us: kernel_blocks(): xin = jnp.swapaxes(inputs, 1, 2).reshape(patch_count * cells, 2 * targets)]
  transfers between devices with their start and end apart: 20 -> 20, of which waited for: 16 -> 16; matrix products, arithmetic and copies ran while one was open for 29% -> 42% of each run, Pallas kernels for 0% -> 0%
where the time goes in v3:
time: 326 us; the launch traced here: 320 us
  local copies, waits for them, and re-layouts  113 us (35%)
  starting transfers between devices  73.8 us (23%)
  other arithmetic  50.2 us (15%)
  waiting for transfers between devices  43.8 us (13%)
  Pallas kernels  28.8 us (9%)
  matrix products  5.4 us (2%)
  between operations  5.18 us (2%)
    concatenate x1, local copies, waits for them, and re-layouts, columns(): jnp.concatenate([shifted(values, row_step, col_step, stride) for row_step...  41.9 us
    ppermute x8, starting transfers between devices, exchange_sum(): other = lax.ppermute(values, axis, route)  30.7 us
    pallas_call x1, Pallas kernels, patch_pass(): pl.pallas_call(patch_kernel, grid=(steps,), in_specs=[block((rows, channe...  28.8 us
    ppermute x8, starting transfers between devices, exchange_sum(): values = kept + lax.ppermute(sent, axis, route)  22.7 us
    ppermute x8, waiting for transfers between devices, exchange_sum(): values = kept + lax.ppermute(sent, axis, route)  19.6 us
    unnamed x54, local copies, waits for them, and re-layouts  15.2 us
    ppermute x8, waiting for transfers between devices, exchange_sum(): other = lax.ppermute(values, axis, route)  14.2 us
    all_to_all x1, starting transfers between devices, per_device(): lax.all_to_all(outgoing, 'rows', split_axis=0, concat_axis=0, tiled=True)  13.6 us
  transfers between devices with their start and end apart: 20, of which 16 were waited for; matrix products, arithmetic and copies ran while one was open for 42% of the time, Pallas kernels for 0%

profile of v3, /device:TPU:1, one launch (start us, length us, event | category | flops | bytes accessed | tf_op | source)
XLA Modules:
  0.0 320.4 jit_solution(4955695704712644876)
XLA Ops:
  1.6 3.9 %collective-permute-start = (bf16[1,100,1,256]{3,1,2,0:T(8,128)(2,1)S(1)}, bf16[1,100,1,256]{3,1,2,0:T(8,128)(2,1)S(1)}, u32[]{:S(2)}, u32[]{:S(2)}) collective-permute-start(bf16[1,100,1,256]{3,1,2,0:T(8,128)(2,1)S(1)} %get-tuple-element.63), channel_id=1, source_target_pairs={{0,4},{4,8},{8,12},{12,16},{16,20},{20,24},{24,28},{28,32},{32,36}... | collective-permute-start | bytes 153608 | tf_op jit(solution)/shard_map/ppermute | solution.py:24
  9.0 9.0 %reduce-window.6 = s32[32,8,128]{2,1,0:T(8,128)S(1)} reduce-window(s32[32,8,128]{2,1,0:T(8,128)S(1)} %fusion.9, s32[]{:T(128)} %constant.284.clone.1), window={size=1x1x128 pad=0_0x0_0x127_0}, to_apply=%region_3.4 | reduce-window | flops 4161536 | bytes 262148 | tf_op jit(solution)/shard_map/reduce-window
  21.2 3.2 %broadcast_select_fusion = bf16[32,2,64,144]{3,2,1,0:T(8,128)(2,1)} fusion(bf16[32,2,64,144]{3,2,1,0:T(8,128)(2,1)} %bitcast.115, pred[32,2]{1,0:T(8,128)(4,1)S(1)} %copy.117), kind=kLoop, calls=%fused_computation.13 | loop fusion | flops 589824 | bytes 2359360 | tf_op jit(solution)/shard_map/jit(_take)/select_n | solution.py:411
  24.4 13.6 %all-to-all-start = ((bf16[32,2,64,144]{3,2,1,0:T(8,128)(2,1)}), bf16[32,2,64,144]{3,2,1,0:T(8,128)(2,1)}, u32[]{:S(2)}, u32[]{:S(2)}) async-start(bf16[32,2,64,144]{3,2,1,0:T(8,128)(2,1)} %broadcast_select_fusion), calls=%async_computation | async-start | bytes 4194304 | tf_op jit(solution)/shard_map/all_to_all | solution.py:413
  45.3 4.4 %slice_select_fusion = (bf16[100,3584]{1,0:T(8,128)(2,1)S(1)}, bf16[100,3584]{1,0:T(8,128)(2,1)S(1)}, bf16[100,3584]{1,0:T(8,128)(2,1)}, bf16[100,3584]{1,0:T(8,...) fusion(pred[3584]{0:T(1024)(128)(4,1)S(1)} %get-tuple-element.7, ...), kind=kLoop, calls=%fused_computation.25 | loop fusion | flops 3225600 | bytes 7178752 | tf_op jit(solution)/shard_map/jit(_where)/select_n | solution.py:48
  49.8 41.9 %concatenate.144 = bf16[900,3584]{1,0:T(8,128)(2,1)} concatenate(bf16[100,3584]{1,0:T(8,128)(2,1)} %get-tuple-element.57, bf16[100,3584]{1,0:T(8,128)(2,1)} %get-tuple-element.60, bf16[100,3584]{1,0:T(8,128)(2,1)} %get-tuple-element.50, bf16[100,3584]{1,0:T(8,128)(2,1)} %get-tuple-element.58, bf16[100,3584]{1,0:T(8,128)(2,1)} %get-tuple-element.61, ...), dimensions={0} | concatenate | bytes 12902400 | tf_op jit(solution)/shard_map/concatenate | solution.py:52
  91.7 5.4 %fusion = bf16[64,3584]{1,0:T(8,128)(2,1)S(1)} fusion(bf16[64,128]{1,0:T(8,128)(2,1)S(1)} %copy-done.19, bf16[900,3584]{1,0:T(8,128)(2,1)} %concatenate.144, bf16[128,900]{0,1:T(8,128)(2,1)S(1)} %copy-done.18), kind=kOutput, calls=%fused_computation.5 | convolution fusion | flops 886996992 | bytes 7156736 | tf_op jit(solution)/shard_map/co,op->cp/dot_general | solution.py:77
  98.9 4.9 %pad_maximum_fusion.1 = bf16[2,64,11,256]{1,0,3,2:T(2,128)(2,1)} fusion(bf16[1,64,12,256]{1,0,3,2:T(2,128)(2,1)S(1)} %copy.107, bf16[1,64,12,256]{1,0,3,2:T(2,128)(2,1)S(1)} %copy.106), kind=kLoop, calls=%fused_computation.15 | loop fusion | flops 1441792 | bytes 1507328 | tf_op jit(solution)/shard_map/stack | solution.py:417
  103.8 4.7 %copy.108 = bf16[2,64,11,256]{3,1,2,0:T(8,128)(2,1)} copy(bf16[2,64,11,256]{1,0,3,2:T(2,128)(2,1)} %pad_maximum_fusion.1) | data formatting | bytes 1441792 | tf_op jit(solution)/shard_map/slice | solution.py:420
  116.9 10.0 %collective-permute-done.2 = bf16[2,64,11,256]{3,1,2,0:T(8,128)(2,1)} collective-permute-done((bf16[2,64,11,256]{3,1,2,0:T(8,128)(2,1)}, bf16[2,64,11,256]{3,1,2,0:T(8,128)(2,1)}, u32[]{:S(2)}, u32[]{:S(2)}) %collective-permute-start.2) | collective-permute-done | bytes 720928 | tf_op jit(solution)/shard_map/ppermute | solution.py:36
  126.9 4.7 %copy.109 = bf16[2,64,11,256]{1,0,3,2:T(2,128)(2,1)} copy(bf16[2,64,11,256]{3,1,2,0:T(8,128)(2,1)} %collective-permute-done.2) | data formatting | bytes 1441792 | tf_op jit(solution)/shard_map/ppermute | solution.py:36
  131.6 8.1 %pad_maximum_fusion = bf16[2,64,23,256]{1,0,3,2:T(2,128)(2,1)} fusion(bf16[2,64,11,256]{1,0,3,2:T(2,128)(2,1)} %copy.109, bf16[1,64,12,256]{1,0,3,2:T(2,128)(2,1)S(1)} %copy.107, bf16[1,64,12,256]{1,0,3,2:T(2,128)(2,1)S(1)} %copy.106), kind=kLoop, calls=%fused_computation.6 | loop fusion | flops 4521984 | bytes 3014656 | tf_op jit(solution)/shard_map/concatenate | solution.py:421
  139.7 8.6 %gather_fusion = bf16[32,2,64,12,12]{2,1,4,3,0:T(2,128)(2,1)S(1)} fusion(bf16[2,64,23,256]{1,0,3,2:T(2,128)(2,1)} %pad_maximum_fusion, s32[32]{0:T(128)S(1)} %get-tuple-element.72), kind=kCustom, calls=%fused_computation | custom fusion | bytes 2359808 | tf_op jit(solution)/shard_map/vmap()/gather | solution.py:388
  148.4 5.4 %fusion.37 = (bf16[32,1,64,144]{2,1,3,0:T(2,128)(2,1)}, bf16[32,1,64,144]{2,1,3,0:T(2,128)(2,1)}) fusion(bf16[32,2,64,144]{2,1,3,0:T(2,128)(2,1)S(1)} %bitcast.110), kind=kLoop, calls=%fused_computation.170 | loop fusion | bytes 2359296 | tf_op jit(solution)/shard_map/slice | solution.py:427
  153.8 4.8 %copy.138 = bf16[32,1,64,144]{3,2,0,1:T(8,128)(2,1)S(1)} copy(bf16[32,1,64,144]{2,1,3,0:T(2,128)(2,1)} %get-tuple-element.45) | data formatting | bytes 1179648
  158.6 3.4 %copy.137 = bf16[32,1,64,144]{3,2,0,1:T(8,128)(2,1)} copy(bf16[32,1,64,144]{2,1,3,0:T(2,128)(2,1)S(1)} %copy-done.2) | data formatting | bytes 1179648
  162.0 3.2 gather_fusion.2
  169.4 3.8 %copy.119 = bf16[32,144,128]{2,1,0:T(8,128)(2,1)} copy(bf16[32,144,128]{1,2,0:T(8,128)(2,1)} %maximum_bitcast_fusion) | data formatting | bytes 2359296 | tf_op jit(solution)/shard_map/transpose | solution.py:304
  178.4 28.8 %shard_map.145 = (f32[4608,64]{1,0:T(8,128)}, f32[32,128]{1,0:T(8,128)}, f32[128,1152]{1,0:T(8,128)}, f32[128,1152]{1,0:T(8,128)}, f32[64,128]{1,0:T(8,128)}) custom-call(bf16[4608,128]{1,0:T(8,128)(2,1)} %bitcast.117, f32[4608,64]{1,0:T(8,128)} %bitcast.111, f32[4608,8]{1,0:T(8,128)} %bitcast.112, f32[4608,128]{1,0:T(8,128)} %bitcast.113, ...), custom_call_target="tpu_custom_call" | custom-call | tf_op jit(solution)/shard_map/pallas_call | solution.py:251
  211.7 2.5 collective-permute-start.3
  218.7 7.2 %collective-permute-done.4 = f32[77312]{0:T(1024)S(1)} collective-permute-done((f32[77312]{0:T(1024)S(1)}, f32[77312]{0:T(1024)S(1)}, u32[]{:S(2)}, u32[]{:S(2)}) %collective-permute-start.4) | collective-permute-done | bytes 309280 | tf_op jit(solution)/shard_map/ppermute | solution.py:360
  227.4 2.8 collective-permute-done.5
  230.2 5.4 %collective-permute-start.6 = (f32[19328]{0:T(1024)S(1)}, f32[19328]{0:T(1024)S(1)}, u32[]{:S(2)}, u32[]{:S(2)}) collective-permute-start(f32[19328]{0:T(1024)S(1)} %slice_select_fusion.10), channel_id=1, source_target_pairs={{0,8},{4,12},{8,0},{12,4},{16,24},{20,28},{24,16},{28,20},{32,40},... | collective-permute-start | bytes 231944 | tf_op jit(solution)/shard_map/ppermute | solution.py:360
  237.5 3.0 collective-permute-start.7
  245.2 2.7 collective-permute-start.9
  249.3 5.1 %collective-permute-start.10 = (f32[1208]{0:T(1024)S(1)}, f32[1208]{0:T(1024)S(1)}, u32[]{:S(2)}, u32[]{:S(2)}) collective-permute-start(f32[1208]{0:T(1024)S(1)} %slice_select_fusion.14), channel_id=1, source_target_pairs={{0,64},{4,68},{8,72},{12,76},{16,80},{20,84},{24,88},{28,92},{32,9... | collective-permute-start | bytes 14504 | tf_op jit(solution)/shard_map/ppermute | solution.py:360
  256.1 4.8 %collective-permute-start.11 = (f32[1208]{0:T(1024)S(1)}, f32[1208]{0:T(1024)S(1)}, u32[]{:S(2)}, u32[]{:S(2)}) collective-permute-start(f32[1208]{0:T(1024)S(1)} %select_add_fusion.7), channel_id=1, source_target_pairs={{0,64},{4,68},{8,72},{12,76},{16,80},{20,84},{24,88},{28,92},{32,9... | collective-permute-start | bytes 14504 | tf_op jit(solution)/shard_map/ppermute | solution.py:365
  269.4 3.0 collective-permute-start.14
  273.9 3.4 %collective-permute-start.15 = (f32[19328]{0:T(1024)S(1)}, f32[19328]{0:T(1024)S(1)}, u32[]{:S(2)}, u32[]{:S(2)}) collective-permute-start(f32[19328]{0:T(1024)S(1)} %maximum_select_fusion.11), channel_id=1, source_target_pairs={{0,8},{4,12},{8,0},{12,4},{16,24},{20,28},{24,16},{28,20},{32,40},... | collective-permute-start | bytes 231944 | tf_op jit(solution)/shard_map/ppermute | solution.py:365
  280.6 3.0 collective-permute-done.16
  285.8 4.0 %collective-permute-done.17 = f32[77312]{0:T(1024)S(1)} collective-permute-done((f32[77312]{0:T(1024)S(1)}, f32[77312]{0:T(1024)S(1)}, u32[]{:S(2)}, u32[]{:S(2)}) %collective-permute-start.17) | collective-permute-done | bytes 309280 | tf_op jit(solution)/shard_map/ppermute | solution.py:365
  289.9 14.4 %collective-permute-start.18 = (f32[154624]{0:T(1024)S(1)}, f32[154624]{0:T(1024)S(1)}, u32[]{:S(2)}, u32[]{:S(2)}) collective-permute-start(f32[154624]{0:T(1024)S(1)} %maximum_select_fusion.3), channel_id=1, source_target_pairs={{0,128},{128,0},{1,129},{129,1},{2,130},{130,2},{3,131},{131,3},{4... | collective-permute-start | bytes 1855496 | tf_op jit(solution)/shard_map/ppermute | solution.py:365
  (197 shorter events, 82.2 us)
Async XLA Ops:
  0.6 18.5 %copy-start = (bf16[1,1,64,64,144]{4,3,2,1,0:T(8,128)(2,1)S(1)}, bf16[1,1,64,64,144]{4,3,2,1,0:T(8,128)(2,1)}, u32[]{:S(2)}) copy-start(bf16[1,1,64,64,144]{4,3,2,1,0:T(8,128)(2,1)} %param.12) | copy-start | bytes 3538948
  1.6 43.0 %collective-permute-start = (bf16[1,100,1,256]{3,1,2,0:T(8,128)(2,1)S(1)}, bf16[1,100,1,256]{3,1,2,0:T(8,128)(2,1)S(1)}, u32[]{:S(2)}, u32[]{:S(2)}) collective-permute-start(bf16[1,100,1,256]{3,1,2,0:T(8,128)(2,1)S(1)} %get-tuple-element.63), channel_id=1, source_target_pairs={{0,4},{4,8},{8,12},{12,16},{16,20},{20,24},{24,28},{28,32},{32,36}... | collective-permute-start | bytes 153608 | tf_op jit(solution)/shard_map/ppermute | solution.py:24
  5.6 39.1 %collective-permute-start.1 = (bf16[1,100,1,256]{3,1,2,0:T(8,128)(2,1)S(1)}, bf16[1,100,1,256]{3,1,2,0:T(8,128)(2,1)S(1)}, u32[]{:S(2)}, u32[]{:S(2)}) collective-permute-start(bf16[1,100,1,256]{3,1,2,0:T(8,128)(2,1)S(1)} %get-tuple-element.64), channel_id=1, source_target_pairs={{4,0},{8,4},{12,8},{16,12},{20,16},{24,20},{28,24},{32,28},{36,32}... | collective-permute-start | bytes 153608 | tf_op jit(solution)/shard_map/ppermute | solution.py:26
  24.4 19.1 %copy-start.6 = (bf16[1,64,12,256]{3,1,2,0:T(8,128)(2,1)S(1)}, bf16[1,64,12,256]{3,1,2,0:T(8,128)(2,1)}, u32[]{:S(2)}) copy-start(bf16[1,64,12,256]{3,1,2,0:T(8,128)(2,1)} %param.11) | copy-start | bytes 1179652
  24.4 20.3 %copy-start.4 = (bf16[1,100,12,256]{3,1,2,0:T(8,128)(2,1)S(1)}, bf16[1,100,12,256]{3,1,2,0:T(8,128)(2,1)}, u32[]{:S(2)}) copy-start(bf16[1,100,12,256]{3,1,2,0:T(8,128)(2,1)} %param.10) | copy-start | bytes 1843204
  24.4 137.6 %all-to-all-start = ((bf16[32,2,64,144]{3,2,1,0:T(8,128)(2,1)}), bf16[32,2,64,144]{3,2,1,0:T(8,128)(2,1)}, u32[]{:S(2)}, u32[]{:S(2)}) async-start(bf16[32,2,64,144]{3,2,1,0:T(8,128)(2,1)} %broadcast_select_fusion), calls=%async_computation | async-start | bytes 4194304 | tf_op jit(solution)/shard_map/all_to_all | solution.py:413
  49.8 41.9 %copy-start.18 = (bf16[128,900]{0,1:T(8,128)(2,1)S(1)}, bf16[128,900]{0,1:T(8,128)(2,1)}, u32[]{:S(2)}) copy-start(bf16[128,900]{0,1:T(8,128)(2,1)} %param.14) | copy-start | bytes 691204
  49.8 41.9 %copy-start.19 = (bf16[64,128]{1,0:T(8,128)(2,1)S(1)}, bf16[64,128]{1,0:T(8,128)(2,1)}, u32[]{:S(2)}) copy-start(bf16[64,128]{1,0:T(8,128)(2,1)} %param.15) | copy-start | bytes 49156
  108.4 7.4 %copy-start.7 = (bf16[64,128]{1,0:T(8,128)(2,1)S(1)}, bf16[64,128]{1,0:T(8,128)(2,1)}, u32[]{:S(2)}) copy-start(bf16[64,128]{1,0:T(8,128)(2,1)} %pm_ref.1) | copy-start | bytes 49156
  108.4 8.1 %copy-start.14 = (s32[32,1]{0,1:T(1,128)S(1)}, s32[32,1]{0,1:T(1,128)}, u32[]{:S(2)}) copy-start(s32[32,1]{0,1:T(1,128)} %get-tuple-element.41) | copy-start | bytes 388
  108.4 8.2 %copy-start.13 = (s32[32]{0:T(128)S(1)}, s32[32]{0:T(128)}, u32[]{:S(2)}) copy-start(s32[32]{0:T(128)} %copy-done.12) | copy-start | bytes 388
  108.4 8.2 %copy-start.9 = (f32[32,128]{1,0:T(8,128)S(1)}, f32[32,128]{1,0:T(8,128)}, u32[]{:S(2)}) copy-start(f32[32,128]{1,0:T(8,128)} %param.19) | copy-start | bytes 49156
  108.5 8.5 %copy-start.16 = (f32[32]{0:T(128)S(1)}, f32[32]{0:T(128)}, u32[]{:S(2)}) copy-start(f32[32]{0:T(128)} %copy-done.15) | copy-start | bytes 388
  108.5 18.5 %collective-permute-start.2 = (bf16[2,64,11,256]{3,1,2,0:T(8,128)(2,1)}, bf16[2,64,11,256]{3,1,2,0:T(8,128)(2,1)}, u32[]{:S(2)}, u32[]{:S(2)}) collective-permute-start(bf16[2,64,11,256]{3,1,2,0:T(8,128)(2,1)} %copy.108), channel_id=1, source_target_pairs={{4,0},{8,4},{12,8},{16,12},{20,16},{24,20},{28,24},{32,28},{36,32}... | collective-permute-start | bytes 2162696 | tf_op jit(solution)/shard_map/ppermute | solution.py:36
  158.6 6.6 %copy-start.11 = (pred[32]{0:T(512)(128)(4,1)S(1)}, pred[32]{0:T(512)(128)(4,1)}, u32[]{:S(2)}) copy-start(pred[32]{0:T(512)(128)(4,1)} %get-tuple-element.40) | copy-start | bytes 100
  211.7 4.3 %collective-permute-start.3 = (f32[154624]{0:T(1024)S(1)}, f32[154624]{0:T(1024)}, u32[]{:S(2)}, u32[]{:S(2)}) collective-permute-start(f32[154624]{0:T(1024)S(1)} %fusion.4), channel_id=1, source_target_pairs={{0,128},{128,0},{1,129},{129,1},{2,130},{130,2},{3,131},{131,3},{4... | collective-permute-start | bytes 1855496 | tf_op jit(solution)/shard_map/ppermute | solution.py:360
  217.3 8.7 %collective-permute-start.4 = (f32[77312]{0:T(1024)S(1)}, f32[77312]{0:T(1024)S(1)}, u32[]{:S(2)}, u32[]{:S(2)}) collective-permute-start(f32[77312]{0:T(1024)S(1)} %slice_select_fusion.8), channel_id=1, source_target_pairs={{0,4},{4,0},{8,12},{12,8},{16,20},{20,16},{24,28},{28,24},{32,36},... | collective-permute-start | bytes 927752 | tf_op jit(solution)/shard_map/ppermute | solution.py:360
  226.0 4.2 %collective-permute-start.5 = (f32[38656]{0:T(1024)S(1)}, f32[38656]{0:T(1024)S(1)}, u32[]{:S(2)}, u32[]{:S(2)}) collective-permute-start(f32[38656]{0:T(1024)S(1)} %slice_select_fusion.9), channel_id=1, source_target_pairs={{0,1},{1,0},{2,3},{3,2},{4,5},{5,4},{6,7},{7,6},{8,9},{9,8},{10,11... | collective-permute-start | bytes 463880 | tf_op jit(solution)/shard_map/ppermute | solution.py:360
  230.2 7.2 %collective-permute-start.6 = (f32[19328]{0:T(1024)S(1)}, f32[19328]{0:T(1024)S(1)}, u32[]{:S(2)}, u32[]{:S(2)}) collective-permute-start(f32[19328]{0:T(1024)S(1)} %slice_select_fusion.10), channel_id=1, source_target_pairs={{0,8},{4,12},{8,0},{12,4},{16,24},{20,28},{24,16},{28,20},{32,40},... | collective-permute-start | bytes 231944 | tf_op jit(solution)/shard_map/ppermute | solution.py:360
  237.5 4.4 %collective-permute-start.7 = (f32[9664]{0:T(1024)S(1)}, f32[9664]{0:T(1024)S(1)}, u32[]{:S(2)}, u32[]{:S(2)}) collective-permute-start(f32[9664]{0:T(1024)S(1)} %slice_select_fusion.11), channel_id=1, source_target_pairs={{0,2},{1,3},{2,0},{3,1},{4,6},{5,7},{6,4},{7,5},{8,10},{9,11},{10,... | collective-permute-start | bytes 115976 | tf_op jit(solution)/shard_map/ppermute | solution.py:360
  242.1 3.0 collective-permute-start.8
  245.2 3.9 %collective-permute-start.9 = (f32[2416]{0:T(1024)S(1)}, f32[2416]{0:T(1024)S(1)}, u32[]{:S(2)}, u32[]{:S(2)}) collective-permute-start(f32[2416]{0:T(1024)S(1)} %slice_select_fusion.13), channel_id=1, source_target_pairs={{0,32},{4,36},{8,40},{12,44},{16,48},{20,52},{24,56},{28,60},{32,0... | collective-permute-start | bytes 29000 | tf_op jit(solution)/shard_map/ppermute | solution.py:360
  249.3 6.7 %collective-permute-start.10 = (f32[1208]{0:T(1024)S(1)}, f32[1208]{0:T(1024)S(1)}, u32[]{:S(2)}, u32[]{:S(2)}) collective-permute-start(f32[1208]{0:T(1024)S(1)} %slice_select_fusion.14), channel_id=1, source_target_pairs={{0,64},{4,68},{8,72},{12,76},{16,80},{20,84},{24,88},{28,92},{32,9... | collective-permute-start | bytes 14504 | tf_op jit(solution)/shard_map/ppermute | solution.py:360
  256.1 6.5 %collective-permute-start.11 = (f32[1208]{0:T(1024)S(1)}, f32[1208]{0:T(1024)S(1)}, u32[]{:S(2)}, u32[]{:S(2)}) collective-permute-start(f32[1208]{0:T(1024)S(1)} %select_add_fusion.7), channel_id=1, source_target_pairs={{0,64},{4,68},{8,72},{12,76},{16,80},{20,84},{24,88},{28,92},{32,9... | collective-permute-start | bytes 14504 | tf_op jit(solution)/shard_map/ppermute | solution.py:365
  262.6 3.5 %collective-permute-start.12 = (f32[2416]{0:T(1024)S(1)}, f32[2416]{0:T(1024)S(1)}, u32[]{:S(2)}, u32[]{:S(2)}) collective-permute-start(f32[2416]{0:T(1024)S(1)} %maximum_select_fusion.14), channel_id=1, source_target_pairs={{0,32},{4,36},{8,40},{12,44},{16,48},{20,52},{24,56},{28,60},{32,0... | collective-permute-start | bytes 29000 | tf_op jit(solution)/shard_map/ppermute | solution.py:365
  266.1 3.2 collective-permute-start.13
  269.4 4.4 %collective-permute-start.14 = (f32[9664]{0:T(1024)S(1)}, f32[9664]{0:T(1024)S(1)}, u32[]{:S(2)}, u32[]{:S(2)}) collective-permute-start(f32[9664]{0:T(1024)S(1)} %maximum_select_fusion.12), channel_id=1, source_target_pairs={{0,2},{1,3},{2,0},{3,1},{4,6},{5,7},{6,4},{7,5},{8,10},{9,11},{10,... | collective-permute-start | bytes 115976 | tf_op jit(solution)/shard_map/ppermute | solution.py:365
  273.9 5.2 %collective-permute-start.15 = (f32[19328]{0:T(1024)S(1)}, f32[19328]{0:T(1024)S(1)}, u32[]{:S(2)}, u32[]{:S(2)}) collective-permute-start(f32[19328]{0:T(1024)S(1)} %maximum_select_fusion.11), channel_id=1, source_target_pairs={{0,8},{4,12},{8,0},{12,4},{16,24},{20,28},{24,16},{28,20},{32,40},... | collective-permute-start | bytes 231944 | tf_op jit(solution)/shard_map/ppermute | solution.py:365
  279.2 4.5 %collective-permute-start.16 = (f32[38656]{0:T(1024)S(1)}, f32[38656]{0:T(1024)S(1)}, u32[]{:S(2)}, u32[]{:S(2)}) collective-permute-start(f32[38656]{0:T(1024)S(1)} %maximum_select_fusion.9), channel_id=1, source_target_pairs={{0,1},{1,0},{2,3},{3,2},{4,5},{5,4},{6,7},{7,6},{8,9},{9,8},{10,11... | collective-permute-start | bytes 463880 | tf_op jit(solution)/shard_map/ppermute | solution.py:365
  283.7 6.1 %collective-permute-start.17 = (f32[77312]{0:T(1024)S(1)}, f32[77312]{0:T(1024)S(1)}, u32[]{:S(2)}, u32[]{:S(2)}) collective-permute-start(f32[77312]{0:T(1024)S(1)} %maximum_select_fusion.5), channel_id=1, source_target_pairs={{0,4},{4,0},{8,12},{12,8},{16,20},{20,16},{24,28},{28,24},{32,36},... | collective-permute-start | bytes 927752 | tf_op jit(solution)/shard_map/ppermute | solution.py:365
  289.9 18.2 %collective-permute-start.18 = (f32[154624]{0:T(1024)S(1)}, f32[154624]{0:T(1024)S(1)}, u32[]{:S(2)}, u32[]{:S(2)}) collective-permute-start(f32[154624]{0:T(1024)S(1)} %maximum_select_fusion.3), channel_id=1, source_target_pairs={{0,128},{128,0},{1,129},{129,1},{2,130},{130,2},{3,131},{131,3},{4... | collective-permute-start | bytes 1855496 | tf_op jit(solution)/shard_map/ppermute | solution.py:365
  311.6 7.4 %copy-start.1 = (bf16[1,1,64,64,144]{4,3,2,1,0:T(8,128)(2,1)S(1)}, bf16[1,1,64,64,144]{4,3,2,1,0:T(8,128)(2,1)}, u32[]{:S(2)}) copy-start(bf16[1,1,64,64,144]{4,3,2,1,0:T(8,128)(2,1)} %param.12) | copy-start | bytes 3538948
  (8 other events, 23.0 us)
